TPU v7x, 32 devices: a whole 2x2x4 slice. The times are simulated.
32 devices in a mesh: dp: 16 (over z, x, core), fsdp: 2 (over y).
Axes of the slice: x: 2, y: 2, z: 4, core: 2. Of those that a mesh axis runs over, the one named last changes fastest.
Arguments:
- inputs: bfloat16 [128, 256, 512], P(('dp', 'fsdp')), may hold values from -0.3125 to 0.3125
- out_grad: bfloat16 [128, 256, 512], P(('dp', 'fsdp')), may hold values from -6 to 6
- coeff_fixed: int32 [128, 16], P(('dp', 'fsdp')), may hold values from 0 to 4096
- atom_counts: int32 [128], P(('dp', 'fsdp')), may hold values from 64 to 256, as said below
- experts: bfloat16 [16, 512, 512], P(None, ('dp', 'fsdp')), may hold values from -0.125 to 0.125
Outputs:
- in_grad: bfloat16 [128, 256, 512], P(('dp', 'fsdp'))
- expert_grad: float32 [16, 512, 512], P(None, ('dp', 'fsdp'))
Inputs may be any that keep to these rules, and one draw needn't show every extreme that they name: `atom_counts`: some system has exactly 256 atoms and some exactly 64.
All inputs are finite; a program needn't handle non-finite values.
Results may differ from a plain program's by a relative error of at most 0.0049.
Values may be sent and summed in bfloat16 or wider, within the bound.
A program may use at most 128 MiB of HBM per device.

v0:
```python
import functools

import jax
import jax.numpy as jnp
from jax import lax
from jax.experimental import pallas as pl
from jax.experimental.pallas import tpu as pltpu
from jax.sharding import PartitionSpec as P

HIGH = lax.Precision.HIGHEST
MESH = pl.DeviceIdType.MESH
BF16 = jnp.bfloat16
F32 = jnp.float32
NEAR_ORDER = (5, 7, 4, 1, 6, 3, 2)


def dot(a, b, ca, cb):
    return lax.dot_general(a, b, (((ca,), (cb,)), ((), ())), preferred_element_type=F32)


def kernel(nz, n_sys, n_exp, rows, width,
           counts_ref, co_ref, in_ref, og_ref, ex_ref,
           ig_ref, eg_ref,
           mk, cl, ca, ka, kt, pb, g, eo, zs, zr, xg, mb, mr,
           loc, ka_s, ka_r, xz_s, xz_r, pb_s, pb_r, zs_s, zs_r, mb_s, mb_r):
    dp = lax.axis_index("dp")
    y = lax.axis_index("fsdp")
    z = dp // 4
    x = lax.rem(dp // 2, 2)
    c = lax.rem(dp, 2)
    me = x * 4 + c * 2 + y
    sr = n_sys * rows
    er_rows = n_exp * rows

    def flip(v, d):
        return lax.rem(v + d, 2)

    def near(j):
        xx, cc, yy = flip(x, j // 4), flip(c, j // 2 % 2), flip(y, j % 2)
        return xx * 4 + cc * 2 + yy, ((z * 2 + xx) * 2 + cc, yy)

    half = z // 2
    zm = z + half * (3 - 2 * z)

    def actual(v):
        return v + half * (3 - 2 * v)

    def line(v):
        return (actual(v) * 2 + x) * 2 + c, y

    def arrival(n):
        return actual((zm, 1 - zm, 2, 3)[n])

    def target(n):
        return actual((3, 2, 1 - zm, zm)[n])

    plane = NEAR_ORDER
    peers = [near(j)[1] for j in plane] + [((lax.rem(z + k, nz) * 2 + x) * 2 + c, y) for k in range(1, nz)]
    barrier = pltpu.get_barrier_semaphore()
    for peer in peers:
        pl.semaphore_signal(barrier, inc=1, device_id=peer, device_id_type=MESH)

    col = lax.broadcasted_iota(jnp.int32, cl.shape[1:], 1)
    row = lax.broadcasted_iota(jnp.int32, cl.shape[1:], 0)
    fixed = jnp.zeros(cl.shape[1:], jnp.int32)
    for s in range(n_sys):
        for e in range(n_exp):
            fixed = jnp.where((row == s) & (col == e), co_ref[s, e], fixed)
    cl[0] = ((fixed >> 6).astype(F32) / 64.0).astype(BF16)
    cl[1] = ((fixed & 63).astype(F32) / 4096.0).astype(BF16)
    pl.semaphore_wait(barrier, len(peers))

    def send(src, dst, s, r, peer):
        copy = pltpu.make_async_remote_copy(
            src_ref=src, dst_ref=dst, send_sem=s, recv_sem=r, device_id=peer, device_id_type=MESH
        )
        copy.start()
        return copy

    n_loc = [0]

    def local(src, dst):
        copy = pltpu.make_async_copy(src, dst, loc.at[n_loc[0]])
        n_loc[0] += 1
        copy.start()
        return copy

    sent = []
    ca_c = [send(cl, ca.at[me], ka_s.at[j - 1], ka_r.at[j - 1], near(j)[1]) for j in plane]
    ca_own = local(cl, ca.at[me])

    def relay(src, block, n, to):
        return pltpu.make_async_remote_copy(
            src_ref=src, dst_ref=xg.at[block], send_sem=xz_s.at[n], recv_sem=xz_r.at[block],
            device_id=to, device_id_type=MESH)

    relay(ex_ref, z, 0, line(1 - zm)).start()

    @pl.when(zm == 1)
    def _():
        relay(ex_ref, z, nz, line(2)).start()

    sent += ca_c

    for s in range(n_sys):
        slot = lax.broadcasted_iota(jnp.int32, og_ref.shape[1:], 0)
        mk[s] = jnp.where(slot < counts_ref[s], og_ref[s], jnp.zeros(og_ref.shape[1:], BF16))
    pb_c, g_own = {}, {}
    for k in range(nz):
        span = 8 * rows
        lanes = pl.ds(pl.multiple_of(target(k) * span, span), span)
        for s in range(n_sys):
            prod = dot(in_ref[s, :, lanes], mk[s], 0, 0).astype(BF16)
            for b in range(8):
                pb[b, k, s * rows:(s + 1) * rows, :] = prod[b * rows:(b + 1) * rows, :]
        for j in plane:
            to, peer = near(j)
            pb_c[k, j] = send(pb.at[to, k], g.at[k, me], pb_s.at[k, j - 1], pb_r.at[k, j - 1], peer)
        g_own[k] = local(pb.at[me, k], g.at[k, me])
    sent += list(pb_c.values())

    mb_c, m_own = {}, {}

    def merge(k, block):
        zz = arrival(k)
        mb[k] = (dot(ka[0], block, 1, 0) + dot(ka[1], block, 1, 0)).astype(BF16).reshape(
            8, n_sys, rows, width)
        for j in plane:
            to, peer = near(j)
            mb_c[k, j] = send(mb.at[k, to], mr.at[:, zz, me], mb_s.at[k, j - 1], mb_r.at[k, j - 1], peer)
            sent.append(mb_c[k, j])
        m_own[k] = local(mb.at[k, me], mr.at[:, zz, me])

    def landed(slot):
        pltpu.make_async_remote_copy(
            src_ref=zs.at[0], dst_ref=zr.at[slot], send_sem=zs_s.at[0], recv_sem=zs_r.at[slot],
            device_id=line(1 - zm), device_id_type=MESH).wait_recv()
        return zr[slot].astype(F32)

    def reduce(k):
        g_own[k].wait()
        for j in plane:
            pb_c[k, j].wait_recv()
        block = g[k].reshape(8 * sr, width)
        eo[k] = dot(kt[0], block, 1, 0) + dot(kt[1], block, 1, 0)

    def onward(k):
        slot = (2 * zm, 1 + 3 * zm, 3)[k]
        return pltpu.make_async_remote_copy(
            src_ref=zs.at[k], dst_ref=zr.at[slot], send_sem=zs_s.at[k], recv_sem=zs_r.at[slot],
            device_id=line((zm + 1, zm + 1, 1 - zm)[k]), device_id_type=MESH)

    def begin(k):
        @pl.when(zm == 0)
        def _():
            zs[k] = eo[k].astype(BF16)
            onward(k).start()

    def proceed(k):
        @pl.when(zm == 1)
        def _():
            zs[k] = (eo[k] + landed(k)).astype(BF16)
            onward(k).start()

    def finish(k):
        m_own[k].wait()
        for j in plane:
            mb_c[k, j].wait_recv()
        zz = arrival(k)
        span = 8 * rows
        lanes = pl.ds(pl.multiple_of(zz * span, span), span)
        for s in range(n_sys):
            ig_ref[s, :, lanes] = dot(mk[s], mr[s, zz].reshape(span, width), 1, 1).astype(BF16)

    ca_own.wait()
    for copy in ca_c:
        copy.wait_recv()
    lane = lax.broadcasted_iota(jnp.int32, (cl.shape[2], er_rows), 1)
    first = lax.broadcasted_iota(jnp.int32, (cl.shape[2], er_rows), 0) * rows
    pick = jnp.where((lane >= first) & (lane < first + rows), 1.0, 0.0).astype(BF16)
    wide = dot(ca[...].reshape(16 * cl.shape[1], cl.shape[2]), pick, 1, 0)
    across = lax.broadcasted_iota(jnp.int32, (rows, er_rows), 1) % rows
    diagonal = across == lax.broadcasted_iota(jnp.int32, (rows, er_rows), 0)
    for p in range(8):
        for h in range(2):
            for s in range(n_sys):
                at = (p * 2 + h) * cl.shape[1] + s
                value = jnp.broadcast_to(wide[at:at + 1, :], (rows, er_rows))
                spot = (p * n_sys + s) * rows
                ka[h, spot:spot + rows, :] = jnp.where(diagonal, value, 0.0).astype(BF16)
    merge(0, ex_ref[...])
    kt[0] = ka[0].T
    kt[1] = ka[1].T

    def arrived(n):
        block = arrival(n)
        copy = relay(ex_ref, block, n, line(1 - zm))
        copy.wait_recv()

        @pl.when(zm == 1)
        def _():
            relay(xg.at[block], block, n, line(2 if n == 1 else 0)).start()

    arrived(1)
    reduce(0)
    begin(0)
    arrived(2)
    merge(1, xg[arrival(1)])
    reduce(1)
    begin(1)
    merge(2, xg[arrival(2)])
    arrived(3)
    proceed(0)
    merge(3, xg[arrival(3)])
    proceed(1)
    reduce(2)
    begin(2)
    proceed(2)
    reduce(3)
    finish(0)
    finish(1)
    finish(2)
    eg_ref[...] = eo[3] + landed(3)

    @pl.when(zm == 1)
    def _():
        eg_ref[...] += landed(4)

    finish(3)
    relay(ex_ref, z, 0, line(1 - zm)).wait_send()
    for k in range(nz - 1):
        onward(k).wait_send()

    @pl.when(zm == 1)
    def _():
        relay(ex_ref, z, nz, line(2)).wait_send()
        for n in range(1, nz):
            relay(ex_ref, z, n, line(0)).wait_send()

    for copy in sent:
        copy.wait_send()


def fused(inputs, out_grad, coeff_fixed, atom_counts, experts, nz):
    n_sys, n_slots, width = inputs.shape
    n_exp, rows, _ = experts.shape
    sr, er_rows = n_sys * rows, n_exp * rows
    vmem = pl.BlockSpec(memory_space=pltpu.VMEM)
    smem = pl.BlockSpec(memory_space=pltpu.SMEM)
    dma = pltpu.SemaphoreType.DMA
    in_grad, expert_grad = pl.pallas_call(
        functools.partial(kernel, nz, n_sys, n_exp, rows, width),
        out_shape=(
            jax.ShapeDtypeStruct(inputs.shape, BF16),
            jax.ShapeDtypeStruct((er_rows, width), F32),
        ),
        in_specs=[smem, smem, vmem, vmem, vmem],
        out_specs=(vmem, vmem),
        scratch_shapes=[
            pltpu.VMEM(out_grad.shape, BF16),
            pltpu.VMEM((2, 16, 128), BF16),
            pltpu.VMEM((8, 2, 16, 128), BF16),
            pltpu.VMEM((2, 8 * sr, er_rows), BF16),
            pltpu.VMEM((2, er_rows, 8 * sr), BF16),
            pltpu.VMEM((8, nz, sr, width), BF16),
            pltpu.VMEM((nz, 8, sr, width), BF16),
            pltpu.VMEM((nz, er_rows, width), F32),
            pltpu.VMEM((nz - 1, er_rows, width), BF16),
            pltpu.VMEM((nz + 1, er_rows, width), BF16),
            pltpu.VMEM((nz, er_rows, width), BF16),
            pltpu.VMEM((nz, 8, n_sys, rows, width), BF16),
            pltpu.VMEM((n_sys, nz, 8, rows, width), BF16),
            dma((1 + 2 * nz,)),
            dma((7,)), dma((7,)), dma((nz + 1,)), dma((nz,)),
            dma((nz, 7)), dma((nz, 7)), dma((nz - 1,)), dma((nz + 1,)),
            dma((nz, 7)), dma((nz, 7)),
        ],
        compiler_params=pltpu.CompilerParams(collective_id=0, has_side_effects=True),
    )(atom_counts, coeff_fixed, inputs, out_grad, experts.reshape(er_rows, width))
    return in_grad, expert_grad.reshape(n_exp, rows, width)


def plain(inputs, out_grad, coeff_fixed, atom_counts, experts):
    both = ("dp", "fsdp")
    n_sys, n_slots, width = inputs.shape
    n_exp, rows, _ = experts.shape
    coeffs = lax.all_gather(coeff_fixed, both, axis=0, tiled=True).astype(F32) / 4096.0
    valid = lax.broadcasted_iota(jnp.int32, (n_sys, n_slots), 1) < atom_counts[:, None]
    masked = jnp.where(valid[:, :, None], out_grad, jnp.zeros_like(out_grad))
    merged = jnp.einsum("se,eij->sij", coeffs, experts.astype(F32), precision=HIGH).astype(BF16)
    merged = lax.all_to_all(merged, both, split_axis=0, concat_axis=1, tiled=True)
    per_system = jnp.einsum("smi,smj->sij", inputs, masked, preferred_element_type=F32)
    per_system = lax.all_to_all(per_system, both, split_axis=1, concat_axis=0, tiled=True)
    expert_grad = jnp.einsum("se,sij->eij", coeffs, per_system, precision=HIGH)
    in_grad = jnp.einsum("smj,sij->smi", masked, merged, preferred_element_type=F32).astype(BF16)
    return in_grad, expert_grad


def solution(mesh):
    n_dp, n_fsdp = mesh.shape["dp"], mesh.shape["fsdp"]

    def shards(inputs, out_grad, coeff_fixed, atom_counts, experts):
        n_sys, _, width = inputs.shape
        n_exp, rows, _ = experts.shape
        if n_dp == 16 and n_fsdp == 2 and rows % 16 == 0 and n_sys <= 16 and n_exp <= 128:
            return fused(inputs, out_grad, coeff_fixed, atom_counts, experts, n_dp // 4)
        return plain(inputs, out_grad, coeff_fixed, atom_counts, experts)

    placed = (
        P(("dp", "fsdp"), None, None),
        P(("dp", "fsdp"), None, None),
        P(("dp", "fsdp"), None),
        P(("dp", "fsdp")),
        P(None, ("dp", "fsdp"), None),
    )
    return jax.shard_map(
        shards,
        mesh=mesh,
        in_specs=placed,
        out_specs=(P(("dp", "fsdp"), None, None), P(None, ("dp", "fsdp"), None)),
        check_vma=False,
    )
```

profile of v0, /device:TPU:0, one launch (start us, length us, event | category | flops | bytes accessed | tf_op | source)
XLA Modules:
  0.0 60.7 jit_solution(7311973009183496785)
XLA Ops:
  0.6 56.9 %shard_map.68 = (bf16[4,256,512]{2,1,0:T(8,128)(2,1)}, f32[256,512]{1,0:T(8,128)}) custom-call(s32[4]{0:T(128)} %counts_ref.1, s32[4,16]{1,0:T(4,128)} %co_ref.1, bf16[4,256,512]{2,1,0:T(8,128)(2,1)} %in_ref.1, bf16[4,256,512]{2,1,0:T(8,128)(2,1)} %og_ref.1, bf16[256,512]{1,0:T(8,128)(2,1)} %bitcast.3), custom_call_target="tpu_custom_call" | custom-call | tf_op jit(solution)/shard_map/pallas_call | solution.py:251
  57.6 0.0 copy-start
  57.6 2.3 %copy.9 = bf16[4,256,512]{2,1,0:T(8,128)(2,1)} copy(bf16[4,256,512]{2,1,0:T(8,128)(2,1)} %get-tuple-element.8) | data formatting | bytes 2097152
  59.9 0.0 copy-done
  59.9 0.8 %copy.10 = f32[16,16,512]{2,1,0:T(8,128)} copy(f32[16,16,512]{2,1,0:T(8,128)S(1)} %bitcast.2) | data formatting | bytes 1048576
Async XLA Ops:
  57.6 2.3 %copy-start = (f32[256,512]{1,0:T(8,128)S(1)}, f32[256,512]{1,0:T(8,128)}, u32[]{:S(2)}) copy-start(f32[256,512]{1,0:T(8,128)} %get-tuple-element.5) | copy-start | bytes 1572868
where the time goes:
time: 60.9 us; the launch traced here: 60.7 us
  Pallas kernels  56.9 us (93%)
  local copies, waits for them, and re-layouts  3.12 us (5%)
  between operations  0.65 us (1%)
    pallas_call x1, Pallas kernels, fused(): pl.pallas_call(functools.partial(kernel, nz, n_sys, n_exp, rows, width),...  56.9 us
    unnamed x4, local copies, waits for them, and re-layouts  3.12 us

commit v1 on v0

v1 whole, which is shorter than its diff:
```python
import functools

import jax
import jax.numpy as jnp
from jax import lax
from jax.experimental import pallas as pl
from jax.experimental.pallas import tpu as pltpu
from jax.sharding import PartitionSpec as P

HIGH = lax.Precision.HIGHEST
MESH = pl.DeviceIdType.MESH
BF16 = jnp.bfloat16
F32 = jnp.float32
NEAR_ORDER = (5, 7, 4, 1, 6, 3, 2)


def dot(a, b, ca, cb):
    return lax.dot_general(a, b, (((ca,), (cb,)), ((), ())), preferred_element_type=F32)


def kernel(nz, n_sys, n_exp, rows, width,
           counts_ref, co_ref, in_ref, og_ref, ex_ref,
           ig_ref, eg_ref,
           mk, cl, ca, ka, kt, kp, kq, pb, g, pc, gc, eo, zs, zr, xg, mb, mc, mr, ps, pr,
           loc, ka_s, ka_r, xp_s, xp_r, xz_s, xz_r, pb_s, pb_r, pc_s, pc_r, zs_s, zs_r,
           mb_s, mb_r, mc_s, mc_r, ps_s, ps_r):
    dp = lax.axis_index("dp")
    y = lax.axis_index("fsdp")
    z = dp // 4
    x = lax.rem(dp // 2, 2)
    c = lax.rem(dp, 2)
    me = x * 4 + c * 2 + y
    sr = n_sys * rows
    half_w = width // 2
    span = 8 * rows
    lo_cols, hi_cols = pl.ds(0, half_w), pl.ds(half_w, half_w)

    def flip(v, d):
        return lax.rem(v + d, 2)

    def place(fx, fc, fy):
        xx, cc, yy = flip(x, fx), flip(c, fc), flip(y, fy)
        return xx * 4 + cc * 2 + yy, ((z * 2 + xx) * 2 + cc, yy)

    def near(j):
        return place(j // 4, j // 2 % 2, j % 2)

    def turned(fp, fq, fc):
        return place(fp * (1 - c) + fq * c, fc, fq * (1 - c) + fp * c)

    p_at = x * (1 - c) + y * c
    q_at = y * (1 - c) + x * c

    half = z // 2
    zm = z + half * (3 - 2 * z)
    mid = zm == 1

    def actual(v):
        return v + half * (3 - 2 * v)

    def line(v):
        return (actual(v) * 2 + x) * 2 + c, y

    def arrival(n):
        return actual((zm, 1 - zm, 2, 3)[n])

    def target(n):
        return actual((3, 2, 1 - zm, zm)[n])

    plane = NEAR_ORDER
    peers = [near(j)[1] for j in plane] + [((lax.rem(z + k, nz) * 2 + x) * 2 + c, y) for k in range(1, nz)]
    barrier = pltpu.get_barrier_semaphore()
    for peer in peers:
        pl.semaphore_signal(barrier, inc=1, device_id=peer, device_id_type=MESH)

    col = lax.broadcasted_iota(jnp.int32, cl.shape[1:], 1)
    row = lax.broadcasted_iota(jnp.int32, cl.shape[1:], 0)
    fixed = jnp.zeros(cl.shape[1:], jnp.int32)
    for s in range(n_sys):
        for e in range(n_exp):
            fixed = jnp.where((row == s) & (col == e), co_ref[s, e], fixed)
    cl[0] = ((fixed >> 6).astype(F32) / 64.0).astype(BF16)
    cl[1] = ((fixed & 63).astype(F32) / 4096.0).astype(BF16)
    pl.semaphore_wait(barrier, len(peers))

    def remote(src, dst, s, r, peer):
        return pltpu.make_async_remote_copy(
            src_ref=src, dst_ref=dst, send_sem=s, recv_sem=r, device_id=peer, device_id_type=MESH
        )

    sent = []

    def send(src, dst, s, r, peer):
        copy = remote(src, dst, s, r, peer)
        copy.start()
        sent.append(copy)
        return copy

    n_loc = [0]

    def local(src, dst):
        copy = pltpu.make_async_copy(src, dst, loc.at[n_loc[0]])
        n_loc[0] += 1
        copy.start()
        return copy

    def own(i):
        return ex_ref.at[:, (lo_cols, hi_cols)[i]] if i < 2 else xg.at[2, z]

    def relay(i, src, block, n, to):
        return remote(src, xg.at[i, block], xz_s.at[i, n], xz_r.at[i, block], to)

    def offer(i):
        relay(i, own(i), z, 0, line(1 - zm)).start()

        @pl.when(mid)
        def _():
            relay(i, own(i), z, nz, line(2)).start()

    xp = send(own(1), xg.at[2, z], xp_s.at[0], xp_r.at[0], turned(1, 0, 0)[1])
    offer(0)
    offer(1)
    ca_c = [send(cl, ca.at[me], ka_s.at[j - 1], ka_r.at[j - 1], near(j)[1]) for j in plane]
    ca_own = local(cl, ca.at[me])

    for s in range(n_sys):
        slot = lax.broadcasted_iota(jnp.int32, og_ref.shape[1:], 0)
        mk[s] = jnp.where(slot < counts_ref[s], og_ref[s], jnp.zeros(og_ref.shape[1:], BF16))

    pb_c, g_own, pc_c, gc_own = {}, {}, {}, {}
    takers = (((0, 0, 0), (1, 0, 0)), ((0, 0, 1), (0, 1, 1)), ((0, 1, 0), (1, 1, 0)), ((1, 0, 1), (1, 1, 1)))

    def produce(k):
        lanes = pl.ds(pl.multiple_of(target(k) * span, span), span)
        for s in range(n_sys):
            prod = dot(in_ref[s, :, lanes], mk[s], 0, 0).astype(BF16)
            for b in range(8):
                pb[b, k, s * rows:(s + 1) * rows, :] = prod[b * rows:(b + 1) * rows, :half_w]
                pc[b, k, s * rows:(s + 1) * rows, :] = prod[b * rows:(b + 1) * rows, half_w:]
        for v in (2, 3, 1):
            at = (p_at if v % 2 else q_at) * 2 + c
            for i in (1, 0):
                src = pc.at[turned(*takers[v][i])[0], k]
                pc_c[k, v, i] = send(src, gc.at[k, i, at], pc_s.at[k, v - 1, i], pc_r.at[k, v - 1, i],
                                     turned(*takers[v][0])[1])
        for j in plane:
            to, peer = near(j)
            pb_c[k, j] = send(pb.at[to, k], g.at[k, me], pb_s.at[k, j - 1], pb_r.at[k, j - 1], peer)
        g_own[k] = local(pb.at[me, k], g.at[k, me])
        for i in range(2):
            gc_own[k, i] = local(pc.at[turned(*takers[0][i])[0], k], gc.at[k, i, q_at * 2 + c])

    mb_c, m_own, mc_c, mc_own = {}, {}, {}, {}

    def merge(k):
        zz = arrival(k)

        def block(i):
            return ex_ref[:, (lo_cols, hi_cols)[i]] if k == 0 and i < 2 else xg[i, zz]

        for i in (1, 2):
            mc[k, i - 1] = (dot(kp[0], block(i), 1, 0) + dot(kp[1], block(i), 1, 0)).astype(BF16).reshape(
                4, n_sys, rows, half_w)
            owner = turned(i - 1, 0, 0)[0]
            for v, (fq, fc) in ((2, (1, 0)), (3, (1, 1)), (1, (0, 1))):
                u = flip(q_at, fq) * 2 + flip(c, fc)
                mc_c[k, v, i] = send(mc.at[k, i - 1, u], mr.at[:, zz, owner, :, hi_cols],
                                     mc_s.at[k, v - 1, i - 1], mc_r.at[k, v - 1, i - 1], turned(0, fq, fc)[1])
            mc_own[k, i] = local(mc.at[k, i - 1, q_at * 2 + c], mr.at[:, zz, owner, :, hi_cols])
        mb[k] = (dot(ka[0], block(0), 1, 0) + dot(ka[1], block(0), 1, 0)).astype(BF16).reshape(
            8, n_sys, rows, half_w)
        for j in plane:
            to, peer = near(j)
            mb_c[k, j] = send(mb.at[k, to], mr.at[:, zz, me, :, lo_cols], mb_s.at[k, j - 1], mb_r.at[k, j - 1], peer)
        m_own[k] = local(mb.at[k, me], mr.at[:, zz, me, :, lo_cols])

    def landed(slot, i):
        remote(zs.at[0, i], zr.at[slot, i], zs_s.at[0, i], zs_r.at[slot, i], line(1 - zm)).wait_recv()
        return zr[slot, i].astype(F32)

    def reduce(k):
        for i in range(2):
            gc_own[k, i].wait()
            for v in (1, 2, 3):
                pc_c[k, v, i].wait_recv()
        for i in (1, 0):
            block = gc[k, i].reshape(4 * sr, half_w)
            eo[k, i + 1] = dot(kq[0], block, 1, 0) + dot(kq[1], block, 1, 0)
            begin(k, i + 1)
        g_own[k].wait()
        for j in plane:
            pb_c[k, j].wait_recv()
        block = g[k].reshape(8 * sr, half_w)
        eo[k, 0] = dot(kt[0], block, 1, 0) + dot(kt[1], block, 1, 0)
        begin(k, 0)

    def onward(k, i):
        slot = (2 * zm, 1 + 3 * zm, 3)[k]
        return remote(zs.at[k, i], zr.at[slot, i], zs_s.at[k, i], zs_r.at[slot, i],
                      line((zm + 1, zm + 1, 1 - zm)[k]))

    def begin(k, i):
        if k < nz - 1:
            @pl.when(zm == 0)
            def _():
                zs[k, i] = eo[k, i].astype(BF16)
                onward(k, i).start()

    def proceed(k, i):
        @pl.when(mid)
        def _():
            zs[k, i] = (eo[k, i] + landed(k, i)).astype(BF16)
            onward(k, i).start()

    def finish(k):
        m_own[k].wait()
        for j in plane:
            mb_c[k, j].wait_recv()
        for i in (1, 2):
            mc_own[k, i].wait()
            for v in (1, 2, 3):
                mc_c[k, v, i].wait_recv()
        zz = arrival(k)
        lanes = pl.ds(pl.multiple_of(zz * span, span), span)
        for s in range(n_sys):
            ig_ref[s, :, lanes] = dot(mk[s], mr[s, zz].reshape(span, width), 1, 1).astype(BF16)

    def came(n, i):
        block = arrival(n)
        relay(i, own(0), block, n, line(1 - zm)).wait_recv()

    def handed(n, i):
        block = arrival(n)

        @pl.when(mid)
        def _():
            came(n, i)
            relay(i, xg.at[i, block], block, n, line(2 if n == 1 else 0)).start()

    def awaited(n):
        @pl.when(zm == 0)
        def _():
            for i in range(3):
                came(n, i)

    produce(0)
    xp.wait_recv()
    offer(2)
    for k in range(1, nz):
        produce(k)

    ca_own.wait()
    for copy in ca_c:
        copy.wait_recv()
    er_rows = n_exp * rows
    lane = lax.broadcasted_iota(jnp.int32, (cl.shape[2], er_rows), 1)
    first = lax.broadcasted_iota(jnp.int32, (cl.shape[2], er_rows), 0) * rows
    pick = jnp.where((lane >= first) & (lane < first + rows), 1.0, 0.0).astype(BF16)
    wide = dot(ca[...].reshape(16 * cl.shape[1], cl.shape[2]), pick, 1, 0)
    across = lax.broadcasted_iota(jnp.int32, (rows, er_rows), 1) % rows
    diagonal = across == lax.broadcasted_iota(jnp.int32, (rows, er_rows), 0)
    for d in range(8):
        for h in range(2):
            for s in range(n_sys):
                at = (d * 2 + h) * cl.shape[1] + s
                value = jnp.broadcast_to(wide[at:at + 1, :], (rows, er_rows))
                spot = (d * n_sys + s) * rows
                ka[h, spot:spot + rows, :] = jnp.where(diagonal, value, 0.0).astype(BF16)
    for h in range(2):
        for u in range(4):
            uq, uc = u // 2, u % 2
            at = (x * (1 - c) + uq * c) * 4 + uc * 2 + uq * (1 - c) + y * c
            kp[h, u * sr:(u + 1) * sr, :] = ka[h, pl.ds(pl.multiple_of(at * sr, sr), sr), :]
    merge(0)
    for h in range(2):
        kt[h] = ka[h].T
        kq[h] = kp[h].T

    for i in range(2):
        handed(1, i)
        handed(2, i)
    reduce(0)
    handed(1, 2)
    handed(2, 2)
    reduce(1)
    awaited(1)
    merge(1)
    handed(3, 0)
    proceed(0, 2)
    handed(3, 1)
    proceed(0, 1)
    reduce(2)
    handed(3, 2)
    proceed(0, 0)
    awaited(2)
    merge(2)
    reduce(3)
    awaited(3)
    merge(3)
    for i in (2, 1, 0):
        proceed(1, i)
        proceed(2, i)
    finish(0)
    finish(1)

    def total(i):
        eo[nz - 1, i] += landed(3, i)

        @pl.when(mid)
        def _():
            eo[nz - 1, i] += landed(4, i)

    total(2)
    ps[...] = eo[nz - 1, 2].astype(BF16)
    ps_c = send(ps, pr, ps_s.at[0], ps_r.at[0], turned(1, 0, 0)[1])
    total(1)
    finish(2)
    total(0)
    eg_ref[:, lo_cols] = eo[nz - 1, 0]
    finish(3)
    ps_c.wait_recv()
    eg_ref[:, hi_cols] = eo[nz - 1, 1] + pr[...].astype(F32)

    for i in range(3):
        relay(i, own(0), z, 0, line(1 - zm)).wait_send()
        for k in range(nz - 1):
            onward(k, i).wait_send()

        @pl.when(mid)
        def _():
            relay(i, own(0), z, nz, line(2)).wait_send()
            for n in range(1, nz):
                relay(i, own(0), z, n, line(0)).wait_send()

    for copy in sent:
        copy.wait_send()


def fused(inputs, out_grad, coeff_fixed, atom_counts, experts, nz):
    n_sys, n_slots, width = inputs.shape
    n_exp, rows, _ = experts.shape
    sr, er_rows = n_sys * rows, n_exp * rows
    half_w = width // 2
    vmem = pl.BlockSpec(memory_space=pltpu.VMEM)
    smem = pl.BlockSpec(memory_space=pltpu.SMEM)
    dma = pltpu.SemaphoreType.DMA
    in_grad, expert_grad = pl.pallas_call(
        functools.partial(kernel, nz, n_sys, n_exp, rows, width),
        out_shape=(
            jax.ShapeDtypeStruct(inputs.shape, BF16),
            jax.ShapeDtypeStruct((er_rows, width), F32),
        ),
        in_specs=[smem, smem, vmem, vmem, vmem],
        out_specs=(vmem, vmem),
        scratch_shapes=[
            pltpu.VMEM(out_grad.shape, BF16),
            pltpu.VMEM((2, 16, 128), BF16),
            pltpu.VMEM((8, 2, 16, 128), BF16),
            pltpu.VMEM((2, 8 * sr, er_rows), BF16),
            pltpu.VMEM((2, er_rows, 8 * sr), BF16),
            pltpu.VMEM((2, 4 * sr, er_rows), BF16),
            pltpu.VMEM((2, er_rows, 4 * sr), BF16),
            pltpu.VMEM((8, nz, sr, half_w), BF16),
            pltpu.VMEM((nz, 8, sr, half_w), BF16),
            pltpu.VMEM((8, nz, sr, half_w), BF16),
            pltpu.VMEM((nz, 2, 4, sr, half_w), BF16),
            pltpu.VMEM((nz, 3, er_rows, half_w), F32),
            pltpu.VMEM((nz - 1, 3, er_rows, half_w), BF16),
            pltpu.VMEM((nz + 1, 3, er_rows, half_w), BF16),
            pltpu.VMEM((3, nz, er_rows, half_w), BF16),
            pltpu.VMEM((nz, 8, n_sys, rows, half_w), BF16),
            pltpu.VMEM((nz, 2, 4, n_sys, rows, half_w), BF16),
            pltpu.VMEM((n_sys, nz, 8, rows, width), BF16),
            pltpu.VMEM((er_rows, half_w), BF16),
            pltpu.VMEM((er_rows, half_w), BF16),
            dma((1 + 6 * nz,)),
            dma((7,)), dma((7,)), dma((1,)), dma((1,)), dma((3, nz + 1)), dma((3, nz)),
            dma((nz, 7)), dma((nz, 7)), dma((nz, 3, 2)), dma((nz, 3, 2)),
            dma((nz - 1, 3)), dma((nz + 1, 3)),
            dma((nz, 7)), dma((nz, 7)), dma((nz, 3, 2)), dma((nz, 3, 2)), dma((1,)), dma((1,)),
        ],
        compiler_params=pltpu.CompilerParams(collective_id=0, has_side_effects=True),
    )(atom_counts, coeff_fixed, inputs, out_grad, experts.reshape(er_rows, width))
    return in_grad, expert_grad.reshape(n_exp, rows, width)


def plain(inputs, out_grad, coeff_fixed, atom_counts, experts):
    both = ("dp", "fsdp")
    n_sys, n_slots, width = inputs.shape
    n_exp, rows, _ = experts.shape
    coeffs = lax.all_gather(coeff_fixed, both, axis=0, tiled=True).astype(F32) / 4096.0
    valid = lax.broadcasted_iota(jnp.int32, (n_sys, n_slots), 1) < atom_counts[:, None]
    masked = jnp.where(valid[:, :, None], out_grad, jnp.zeros_like(out_grad))
    merged = jnp.einsum("se,eij->sij", coeffs, experts.astype(F32), precision=HIGH).astype(BF16)
    merged = lax.all_to_all(merged, both, split_axis=0, concat_axis=1, tiled=True)
    per_system = jnp.einsum("smi,smj->sij", inputs, masked, preferred_element_type=F32)
    per_system = lax.all_to_all(per_system, both, split_axis=1, concat_axis=0, tiled=True)
    expert_grad = jnp.einsum("se,sij->eij", coeffs, per_system, precision=HIGH)
    in_grad = jnp.einsum("smj,sij->smi", masked, merged, preferred_element_type=F32).astype(BF16)
    return in_grad, expert_grad


def solution(mesh):
    n_dp, n_fsdp = mesh.shape["dp"], mesh.shape["fsdp"]

    def shards(inputs, out_grad, coeff_fixed, atom_counts, experts):
        n_sys, _, width = inputs.shape
        n_exp, rows, _ = experts.shape
        if n_dp == 16 and n_fsdp == 2 and rows % 16 == 0 and n_sys <= 16 and n_exp <= 128 and width % 256 == 0:
            return fused(inputs, out_grad, coeff_fixed, atom_counts, experts, n_dp // 4)
        return plain(inputs, out_grad, coeff_fixed, atom_counts, experts)

    placed = (
        P(("dp", "fsdp"), None, None),
        P(("dp", "fsdp"), None, None),
        P(("dp", "fsdp"), None),
        P(("dp", "fsdp")),
        P(None, ("dp", "fsdp"), None),
    )
    return jax.shard_map(
        shards,
        mesh=mesh,
        in_specs=placed,
        out_specs=(P(("dp", "fsdp"), None, None), P(None, ("dp", "fsdp"), None)),
        check_vma=False,
    )
```

time: 60.9 us -> 54.7 us (0.90)
  Pallas kernels: 56.9 us -> 50.8 us
    pallas_call x1, Pallas kernels: 56.9 us -> 50.8 us  [fused(): pl.pallas_call(functools.partial(kernel, nz, n_sys, n_exp, rows, width),...]
where the time goes in v1:
time: 54.7 us; the launch traced here: 54.5 us
  Pallas kernels  50.8 us (93%)
  local copies, waits for them, and re-layouts  3.12 us (6%)
  between operations  0.65 us (1%)
    pallas_call x1, Pallas kernels, fused(): pl.pallas_call(functools.partial(kernel, nz, n_sys, n_exp, rows, width),...  50.8 us
    unnamed x4, local copies, waits for them, and re-layouts  3.12 us

profile of v1, /device:TPU:0, one launch (start us, length us, event | category | flops | bytes accessed | tf_op | source)
XLA Modules:
  0.0 54.5 jit_solution(16354217424445813843)
XLA Ops:
  0.6 50.8 %shard_map.68 = (bf16[4,256,512]{2,1,0:T(8,128)(2,1)}, f32[256,512]{1,0:T(8,128)}) custom-call(s32[4]{0:T(128)} %counts_ref.1, s32[4,16]{1,0:T(4,128)} %co_ref.1, bf16[4,256,512]{2,1,0:T(8,128)(2,1)} %in_ref.1, bf16[4,256,512]{2,1,0:T(8,128)(2,1)} %og_ref.1, bf16[256,512]{1,0:T(8,128)(2,1)} %bitcast.3), custom_call_target="tpu_custom_call" | custom-call | tf_op jit(solution)/shard_map/pallas_call | solution.py:347
  51.4 0.0 copy-start
  51.4 2.3 %copy.9 = bf16[4,256,512]{2,1,0:T(8,128)(2,1)} copy(bf16[4,256,512]{2,1,0:T(8,128)(2,1)} %get-tuple-element.8) | data formatting | bytes 2097152
  53.7 0.0 copy-done
  53.7 0.8 %copy.10 = f32[16,16,512]{2,1,0:T(8,128)} copy(f32[16,16,512]{2,1,0:T(8,128)S(1)} %bitcast.2) | data formatting | bytes 1048576
Async XLA Ops:
  51.4 2.3 %copy-start = (f32[256,512]{1,0:T(8,128)S(1)}, f32[256,512]{1,0:T(8,128)}, u32[]{:S(2)}) copy-start(f32[256,512]{1,0:T(8,128)} %get-tuple-element.5) | copy-start | bytes 1572868

commit v2 on v1

--- a/solution.py
+++ b/solution.py
@@ -19,10 +19,10 @@
 
 
 def kernel(nz, n_sys, n_exp, rows, width,
-           counts_ref, co_ref, in_ref, og_ref, ex_ref,
+           counts_hbm, co_hbm, in_hbm, og_hbm, ex_hbm,
            ig_ref, eg_ref,
-           mk, cl, ca, ka, kt, kp, kq, pb, g, pc, gc, eo, zs, zr, xg, mb, mc, mr, ps, pr,
-           loc, ka_s, ka_r, xp_s, xp_r, xz_s, xz_r, pb_s, pb_r, pc_s, pc_r, zs_s, zs_r,
+           counts_ref, co_ref, in_ref, ex_ref, mk, cl, ca, ka, kt, kp, kq, pb, g, pc, gc, eo, zs, zr, xg, mb, mc, mr, ps, pr,
+           ld, loc, ka_s, ka_r, xp_s, xp_r, xz_s, xz_r, pb_s, pb_r, pc_s, pc_r, zs_s, zs_r,
            mb_s, mb_r, mc_s, mc_r, ps_s, ps_r):
     dp = lax.axis_index("dp")
     y = lax.axis_index("fsdp")
@@ -73,14 +73,28 @@
     for peer in peers:
         pl.semaphore_signal(barrier, inc=1, device_id=peer, device_id_type=MESH)
 
+    def load(n, src, dst):
+        copy = pltpu.make_async_copy(src, dst, ld.at[n])
+        copy.start()
+        return copy
+
+    co_c = load(1 + 2 * n_sys, co_hbm, co_ref)
+    counts_c = load(2 + 2 * n_sys, counts_hbm, counts_ref)
+    ex_c = load(0, ex_hbm, ex_ref)
+    og_c = [load(1 + s, og_hbm.at[s], mk.at[s]) for s in range(n_sys)]
+    in_c = [load(1 + n_sys + s, in_hbm.at[s], in_ref.at[s]) for s in range(n_sys)]
+
     col = lax.broadcasted_iota(jnp.int32, cl.shape[1:], 1)
     row = lax.broadcasted_iota(jnp.int32, cl.shape[1:], 0)
     fixed = jnp.zeros(cl.shape[1:], jnp.int32)
+    co_c.wait()
+    counts_c.wait()
     for s in range(n_sys):
         for e in range(n_exp):
             fixed = jnp.where((row == s) & (col == e), co_ref[s, e], fixed)
     cl[0] = ((fixed >> 6).astype(F32) / 64.0).astype(BF16)
     cl[1] = ((fixed & 63).astype(F32) / 4096.0).astype(BF16)
+    ex_c.wait()
     pl.semaphore_wait(barrier, len(peers))
 
     def remote(src, dst, s, r, peer):
@@ -124,8 +138,11 @@
     ca_own = local(cl, ca.at[me])
 
     for s in range(n_sys):
-        slot = lax.broadcasted_iota(jnp.int32, og_ref.shape[1:], 0)
-        mk[s] = jnp.where(slot < counts_ref[s], og_ref[s], jnp.zeros(og_ref.shape[1:], BF16))
+        og_c[s].wait()
+        slot = lax.broadcasted_iota(jnp.int32, mk.shape[1:], 0)
+        mk[s] = jnp.where(slot < counts_ref[s], mk[s], jnp.zeros(mk.shape[1:], BF16))
+    for copy in in_c:
+        copy.wait()
 
     pb_c, g_own, pc_c, gc_own = {}, {}, {}, {}
     takers = (((0, 0, 0), (1, 0, 0)), ((0, 0, 1), (0, 1, 1)), ((0, 1, 0), (1, 1, 0)), ((1, 0, 1), (1, 1, 1)))
@@ -336,23 +353,35 @@
         copy.wait_send()
 
 
+def settle(ig_ref, eg_ref, ig_hbm, eg_hbm, done):
+    copies = [pltpu.make_async_copy(ig_ref, ig_hbm, done.at[0]), pltpu.make_async_copy(eg_ref, eg_hbm, done.at[1])]
+    for copy in copies:
+        copy.start()
+    for copy in copies:
+        copy.wait()
+
+
 def fused(inputs, out_grad, coeff_fixed, atom_counts, experts, nz):
     n_sys, n_slots, width = inputs.shape
     n_exp, rows, _ = experts.shape
     sr, er_rows = n_sys * rows, n_exp * rows
     half_w = width // 2
     vmem = pl.BlockSpec(memory_space=pltpu.VMEM)
-    smem = pl.BlockSpec(memory_space=pltpu.SMEM)
+    hbm = pl.BlockSpec(memory_space=pltpu.HBM)
     dma = pltpu.SemaphoreType.DMA
     in_grad, expert_grad = pl.pallas_call(
         functools.partial(kernel, nz, n_sys, n_exp, rows, width),
         out_shape=(
-            jax.ShapeDtypeStruct(inputs.shape, BF16),
-            jax.ShapeDtypeStruct((er_rows, width), F32),
+            pltpu.VMEM(inputs.shape, BF16),
+            pltpu.VMEM((er_rows, width), F32),
         ),
-        in_specs=[smem, smem, vmem, vmem, vmem],
+        in_specs=[hbm] * 5,
         out_specs=(vmem, vmem),
         scratch_shapes=[
+            pltpu.SMEM(atom_counts.shape, jnp.int32),
+            pltpu.SMEM(coeff_fixed.shape, jnp.int32),
+            pltpu.VMEM(inputs.shape, BF16),
+            pltpu.VMEM((er_rows, width), BF16),
             pltpu.VMEM(out_grad.shape, BF16),
             pltpu.VMEM((2, 16, 128), BF16),
             pltpu.VMEM((8, 2, 16, 128), BF16),
@@ -373,14 +402,29 @@
             pltpu.VMEM((n_sys, nz, 8, rows, width), BF16),
             pltpu.VMEM((er_rows, half_w), BF16),
             pltpu.VMEM((er_rows, half_w), BF16),
-            dma((1 + 6 * nz,)),
+            dma((3 + 2 * n_sys,)), dma((1 + 6 * nz,)),
             dma((7,)), dma((7,)), dma((1,)), dma((1,)), dma((3, nz + 1)), dma((3, nz)),
             dma((nz, 7)), dma((nz, 7)), dma((nz, 3, 2)), dma((nz, 3, 2)),
             dma((nz - 1, 3)), dma((nz + 1, 3)),
             dma((nz, 7)), dma((nz, 7)), dma((nz, 3, 2)), dma((nz, 3, 2)), dma((1,)), dma((1,)),
         ],
-        compiler_params=pltpu.CompilerParams(collective_id=0, has_side_effects=True),
-    )(atom_counts, coeff_fixed, inputs, out_grad, experts.reshape(er_rows, width))
+        compiler_params=pltpu.CompilerParams(
+            collective_id=0, has_side_effects=True, vmem_limit_bytes=48 * 1024 * 1024),
+    )(*(
+        pltpu.with_memory_space_constraint(a, pltpu.HBM)
+        for a in (atom_counts, coeff_fixed, inputs, out_grad, experts.reshape(er_rows, width))))
+    held = [pltpu.with_memory_space_constraint(a, pltpu.VMEM) for a in (in_grad, expert_grad)]
+    in_grad, expert_grad = pl.pallas_call(
+        settle,
+        out_shape=(
+            jax.ShapeDtypeStruct(inputs.shape, BF16),
+            jax.ShapeDtypeStruct((er_rows, width), F32),
+        ),
+        in_specs=[vmem, vmem],
+        out_specs=(hbm, hbm),
+        scratch_shapes=[dma((2,))],
+        compiler_params=pltpu.CompilerParams(vmem_limit_bytes=16 * 1024 * 1024),
+    )(*held)
     return in_grad, expert_grad.reshape(n_exp, rows, width)
 
 

time: 54.7 us -> 50.3 us (0.920)
  local copies, waits for them, and re-layouts: 3.12 us -> 0 us
  Pallas kernels: 50.8 us -> 49.5 us
    unnamed x4 -> x0, local copies, waits for them, and re-layouts: 3.12 us -> none
    pallas_call x1, Pallas kernels: 50.8 us -> 48.3 us  [fused(): pl.pallas_call(functools.partial(kernel, nz, n_sys, n_exp, rows, width),...]
    pallas_call x0 -> x1, Pallas kernels: none -> 1.16 us  [fused(): pl.pallas_call(settle, out_shape=(jax.ShapeDtypeStruct(inputs.shape, BF16...]
where the time goes in v2:
time: 50.3 us; the launch traced here: 50.1 us
  Pallas kernels  49.5 us (98%)
  between operations  0.64 us (1%)
    pallas_call x1, Pallas kernels, fused(): pl.pallas_call(functools.partial(kernel, nz, n_sys, n_exp, rows, width),...  48.3 us
    pallas_call x1, Pallas kernels, fused(): pl.pallas_call(settle, out_shape=(jax.ShapeDtypeStruct(inputs.shape, BF16...  1.16 us

profile of v2, /device:TPU:0, one launch (start us, length us, event | category | flops | bytes accessed | tf_op | source)
XLA Modules:
  0.0 50.1 jit_solution(2095032063213543142)
XLA Ops:
  0.6 48.3 %shard_map.68 = (bf16[4,256,512]{2,1,0:T(8,128)(2,1)S(1)}, f32[256,512]{1,0:T(8,128)S(1)}) custom-call(s32[4]{0:T(128)} %counts_hbm.1, s32[4,16]{1,0:T(4,128)} %co_hbm.1, bf16[4,256,512]{2,1,0:T(8,128)(2,1)} %in_hbm.1, bf16[4,256,512]{2,1,0:T(8,128)(2,1)} %og_hbm.1, bf16[256,512]{1,0:T(8,128)(2,1)} %bitcast.2), custom_call_target="tpu_custom_call" | custom-call | tf_op jit(solution)/shard_map/pallas_call | solution.py:372
  49.0 1.2 %shard_map.69 = (bf16[4,256,512]{2,1,0:T(8,128)(2,1)}, f32[256,512]{1,0:T(8,128)}) custom-call(bf16[4,256,512]{2,1,0:T(8,128)(2,1)S(1)} %get-tuple-element.6.ig_ref, f32[256,512]{1,0:T(8,128)S(1)} %get-tuple-element.7.eg_ref), custom_call_target="tpu_custom_call" | custom-call | tf_op jit(solution)/shard_map/pallas_call | solution.py:417

commit v3 on v2

--- a/solution.py
+++ b/solution.py
@@ -21,7 +21,7 @@
 def kernel(nz, n_sys, n_exp, rows, width,
            counts_hbm, co_hbm, in_hbm, og_hbm, ex_hbm,
            ig_ref, eg_ref,
-           counts_ref, co_ref, in_ref, ex_ref, mk, cl, ca, ka, kt, kp, kq, pb, g, pc, gc, eo, zs, zr, xg, mb, mc, mr, ps, pr,
+           counts_ref, co_ref, in_ref, ex_ref, mk, cl, ca, ka, kt, kp, kq, pb, g, pc, gc, eo, zs, zr, xg, mb, mc, mr, mq, ps, pr,
            ld, loc, ka_s, ka_r, xp_s, xp_r, xz_s, xz_r, pb_s, pb_r, pc_s, pc_r, zs_s, zs_r,
            mb_s, mb_r, mc_s, mc_r, ps_s, ps_r):
     dp = lax.axis_index("dp")
@@ -68,10 +68,14 @@
         return actual((3, 2, 1 - zm, zm)[n])
 
     plane = NEAR_ORDER
-    peers = [near(j)[1] for j in plane] + [((lax.rem(z + k, nz) * 2 + x) * 2 + c, y) for k in range(1, nz)]
+    peers = [near(j)[1] for j in plane] + [line(1 - zm)]
     barrier = pltpu.get_barrier_semaphore()
     for peer in peers:
         pl.semaphore_signal(barrier, inc=1, device_id=peer, device_id_type=MESH)
+
+    @pl.when(mid)
+    def _():
+        pl.semaphore_signal(barrier, inc=1, device_id=line(2), device_id_type=MESH)
 
     def load(n, src, dst):
         copy = pltpu.make_async_copy(src, dst, ld.at[n])
@@ -95,7 +99,7 @@
     cl[0] = ((fixed >> 6).astype(F32) / 64.0).astype(BF16)
     cl[1] = ((fixed & 63).astype(F32) / 4096.0).astype(BF16)
     ex_c.wait()
-    pl.semaphore_wait(barrier, len(peers))
+    pl.semaphore_wait(barrier, len(peers) + zm)
 
     def remote(src, dst, s, r, peer):
         return pltpu.make_async_remote_copy(
@@ -145,7 +149,12 @@
         copy.wait()
 
     pb_c, g_own, pc_c, gc_own = {}, {}, {}, {}
-    takers = (((0, 0, 0), (1, 0, 0)), ((0, 0, 1), (0, 1, 1)), ((0, 1, 0), (1, 1, 0)), ((1, 0, 1), (1, 1, 1)))
+    takers = ((0, 0, 0), (0, 0, 1), (0, 1, 0), (1, 0, 1))
+
+    def seat(b):
+        fx, fc, fy = flip(x, b // 4), flip(c, b // 2 % 2), flip(y, b % 2)
+        fp, fq = fx * (1 - c) + fy * c, fy * (1 - c) + fx * c
+        return (1 - fc) * (4 * fq + fp) + fc * (2 + 4 * fp + fq)
 
     def produce(k):
         lanes = pl.ds(pl.multiple_of(target(k) * span, span), span)
@@ -153,60 +162,64 @@
             prod = dot(in_ref[s, :, lanes], mk[s], 0, 0).astype(BF16)
             for b in range(8):
                 pb[b, k, s * rows:(s + 1) * rows, :] = prod[b * rows:(b + 1) * rows, :half_w]
-                pc[b, k, s * rows:(s + 1) * rows, :] = prod[b * rows:(b + 1) * rows, half_w:]
+                pc[k, seat(b), s * rows:(s + 1) * rows, :] = prod[b * rows:(b + 1) * rows, half_w:]
         for v in (2, 3, 1):
             at = (p_at if v % 2 else q_at) * 2 + c
-            for i in (1, 0):
-                src = pc.at[turned(*takers[v][i])[0], k]
-                pc_c[k, v, i] = send(src, gc.at[k, i, at], pc_s.at[k, v - 1, i], pc_r.at[k, v - 1, i],
-                                     turned(*takers[v][0])[1])
+            pc_c[k, v] = send(pc.at[k, 2 * v:2 * v + 2], gc.at[k, :, at], pc_s.at[k, v - 1], pc_r.at[k, v - 1],
+                              turned(*takers[v])[1])
+        gc_own[k] = local(pc.at[k, 0:2], gc.at[k, :, q_at * 2 + c])
+
+    def deal(h):
+        two = slice(2 * h, 2 * h + 2)
         for j in plane:
             to, peer = near(j)
-            pb_c[k, j] = send(pb.at[to, k], g.at[k, me], pb_s.at[k, j - 1], pb_r.at[k, j - 1], peer)
-        g_own[k] = local(pb.at[me, k], g.at[k, me])
-        for i in range(2):
-            gc_own[k, i] = local(pc.at[turned(*takers[0][i])[0], k], gc.at[k, i, q_at * 2 + c])
+            pb_c[h, j] = send(pb.at[to, two], g.at[two, me], pb_s.at[h, j - 1], pb_r.at[h, j - 1], peer)
+        g_own[h] = local(pb.at[me, two], g.at[two, me])
 
     mb_c, m_own, mc_c, mc_own = {}, {}, {}, {}
 
-    def merge(k):
-        zz = arrival(k)
-
-        def block(i):
-            return ex_ref[:, (lo_cols, hi_cols)[i]] if k == 0 and i < 2 else xg[i, zz]
-
-        for i in (1, 2):
-            mc[k, i - 1] = (dot(kp[0], block(i), 1, 0) + dot(kp[1], block(i), 1, 0)).astype(BF16).reshape(
-                4, n_sys, rows, half_w)
-            owner = turned(i - 1, 0, 0)[0]
-            for v, (fq, fc) in ((2, (1, 0)), (3, (1, 1)), (1, (0, 1))):
-                u = flip(q_at, fq) * 2 + flip(c, fc)
-                mc_c[k, v, i] = send(mc.at[k, i - 1, u], mr.at[:, zz, owner, :, hi_cols],
-                                     mc_s.at[k, v - 1, i - 1], mc_r.at[k, v - 1, i - 1], turned(0, fq, fc)[1])
-            mc_own[k, i] = local(mc.at[k, i - 1, q_at * 2 + c], mr.at[:, zz, owner, :, hi_cols])
-        mb[k] = (dot(ka[0], block(0), 1, 0) + dot(ka[1], block(0), 1, 0)).astype(BF16).reshape(
-            8, n_sys, rows, half_w)
+    def held(k, i):
+        return ex_ref[:, (lo_cols, hi_cols)[i]] if k == 0 and i < 2 else xg[i, arrival(k)]
+
+    def merge(*ks):
+        span_k = slice(ks[0], ks[-1] + 1)
+        for k in ks:
+            for i in (1, 2):
+                piece = held(k, i)
+                mc[:, :, k, flip(p_at, i - 1)] = (dot(kp[0], piece, 1, 0) + dot(kp[1], piece, 1, 0)).astype(
+                    BF16).reshape(4, n_sys, rows, half_w)
+        k = ks[-1]
+        at = 2 * c + q_at
+        for v, (fq, fc) in ((2, (1, 0)), (3, (1, 1)), (1, (0, 1))):
+            u = flip(q_at, fq) * 2 + flip(c, fc)
+            mc_c[k, v] = send(mc.at[u, :, span_k], mq.at[:, span_k, at], mc_s.at[k, v - 1], mc_r.at[k, v - 1],
+                              turned(0, fq, fc)[1])
+        mc_own[k] = local(mc.at[q_at * 2 + c, :, span_k], mq.at[:, span_k, at])
+        for k in ks:
+            piece = held(k, 0)
+            mb[:, :, k] = (dot(ka[0], piece, 1, 0) + dot(ka[1], piece, 1, 0)).astype(BF16).reshape(
+                8, n_sys, rows, half_w)
         for j in plane:
             to, peer = near(j)
-            mb_c[k, j] = send(mb.at[k, to], mr.at[:, zz, me, :, lo_cols], mb_s.at[k, j - 1], mb_r.at[k, j - 1], peer)
-        m_own[k] = local(mb.at[k, me], mr.at[:, zz, me, :, lo_cols])
+            mb_c[k, j] = send(mb.at[to, :, span_k], mr.at[:, span_k, me], mb_s.at[k, j - 1], mb_r.at[k, j - 1], peer)
+        m_own[k] = local(mb.at[me, :, span_k], mr.at[:, span_k, me])
 
     def landed(slot, i):
         remote(zs.at[0, i], zr.at[slot, i], zs_s.at[0, i], zs_r.at[slot, i], line(1 - zm)).wait_recv()
         return zr[slot, i].astype(F32)
 
     def reduce(k):
-        for i in range(2):
-            gc_own[k, i].wait()
-            for v in (1, 2, 3):
-                pc_c[k, v, i].wait_recv()
+        gc_own[k].wait()
+        for v in (1, 2, 3):
+            pc_c[k, v].wait_recv()
         for i in (1, 0):
             block = gc[k, i].reshape(4 * sr, half_w)
             eo[k, i + 1] = dot(kq[0], block, 1, 0) + dot(kq[1], block, 1, 0)
             begin(k, i + 1)
-        g_own[k].wait()
-        for j in plane:
-            pb_c[k, j].wait_recv()
+        if k % 2 == 0:
+            g_own[k // 2].wait()
+            for j in plane:
+                pb_c[k // 2, j].wait_recv()
         block = g[k].reshape(8 * sr, half_w)
         eo[k, 0] = dot(kt[0], block, 1, 0) + dot(kt[1], block, 1, 0)
         begin(k, 0)
@@ -230,17 +243,19 @@
             onward(k, i).start()
 
     def finish(k):
-        m_own[k].wait()
-        for j in plane:
-            mb_c[k, j].wait_recv()
-        for i in (1, 2):
-            mc_own[k, i].wait()
+        if k in m_own:
+            m_own[k].wait()
+            mc_own[k].wait()
+            for j in plane:
+                mb_c[k, j].wait_recv()
             for v in (1, 2, 3):
-                mc_c[k, v, i].wait_recv()
-        zz = arrival(k)
-        lanes = pl.ds(pl.multiple_of(zz * span, span), span)
+                mc_c[k, v].wait_recv()
+        lanes = pl.ds(pl.multiple_of(arrival(k) * span, span), span)
         for s in range(n_sys):
-            ig_ref[s, :, lanes] = dot(mk[s], mr[s, zz].reshape(span, width), 1, 1).astype(BF16)
+            first = mr[s, k].reshape(span, half_w)
+            last = jnp.concatenate([mq[s, k, (b % 2, 2 + b // 4)[b // 2 % 2], (b // 4, b % 2)[b // 2 % 2]]
+                                    for b in range(8)], axis=0)
+            ig_ref[s, :, lanes] = dot(mk[s], jnp.concatenate([first, last], axis=1), 1, 1).astype(BF16)
 
     def came(n, i):
         block = arrival(n)
@@ -263,8 +278,11 @@
     produce(0)
     xp.wait_recv()
     offer(2)
-    for k in range(1, nz):
-        produce(k)
+    produce(1)
+    deal(0)
+    produce(2)
+    produce(3)
+    deal(1)
 
     ca_own.wait()
     for copy in ca_c:
@@ -288,7 +306,6 @@
             uq, uc = u // 2, u % 2
             at = (x * (1 - c) + uq * c) * 4 + uc * 2 + uq * (1 - c) + y * c
             kp[h, u * sr:(u + 1) * sr, :] = ka[h, pl.ds(pl.multiple_of(at * sr, sr), sr), :]
-    merge(0)
     for h in range(2):
         kt[h] = ka[h].T
         kq[h] = kp[h].T
@@ -301,7 +318,7 @@
     handed(2, 2)
     reduce(1)
     awaited(1)
-    merge(1)
+    merge(0, 1)
     handed(3, 0)
     proceed(0, 2)
     handed(3, 1)
@@ -317,8 +334,8 @@
     for i in (2, 1, 0):
         proceed(1, i)
         proceed(2, i)
+    finish(1)
     finish(0)
-    finish(1)
 
     def total(i):
         eo[nz - 1, i] += landed(3, i)
@@ -391,22 +408,23 @@
             pltpu.VMEM((2, er_rows, 4 * sr), BF16),
             pltpu.VMEM((8, nz, sr, half_w), BF16),
             pltpu.VMEM((nz, 8, sr, half_w), BF16),
-            pltpu.VMEM((8, nz, sr, half_w), BF16),
+            pltpu.VMEM((nz, 8, sr, half_w), BF16),
             pltpu.VMEM((nz, 2, 4, sr, half_w), BF16),
             pltpu.VMEM((nz, 3, er_rows, half_w), F32),
             pltpu.VMEM((nz - 1, 3, er_rows, half_w), BF16),
             pltpu.VMEM((nz + 1, 3, er_rows, half_w), BF16),
             pltpu.VMEM((3, nz, er_rows, half_w), BF16),
-            pltpu.VMEM((nz, 8, n_sys, rows, half_w), BF16),
-            pltpu.VMEM((nz, 2, 4, n_sys, rows, half_w), BF16),
-            pltpu.VMEM((n_sys, nz, 8, rows, width), BF16),
+            pltpu.VMEM((8, n_sys, nz, rows, half_w), BF16),
+            pltpu.VMEM((4, n_sys, nz, 2, rows, half_w), BF16),
+            pltpu.VMEM((n_sys, nz, 8, rows, half_w), BF16),
+            pltpu.VMEM((n_sys, nz, 4, 2, rows, half_w), BF16),
             pltpu.VMEM((er_rows, half_w), BF16),
             pltpu.VMEM((er_rows, half_w), BF16),
-            dma((3 + 2 * n_sys,)), dma((1 + 6 * nz,)),
+            dma((3 + 2 * n_sys,)), dma((1 + 4 * nz,)),
             dma((7,)), dma((7,)), dma((1,)), dma((1,)), dma((3, nz + 1)), dma((3, nz)),
-            dma((nz, 7)), dma((nz, 7)), dma((nz, 3, 2)), dma((nz, 3, 2)),
+            dma((nz // 2, 7)), dma((nz // 2, 7)), dma((nz, 3)), dma((nz, 3)),
             dma((nz - 1, 3)), dma((nz + 1, 3)),
-            dma((nz, 7)), dma((nz, 7)), dma((nz, 3, 2)), dma((nz, 3, 2)), dma((1,)), dma((1,)),
+            dma((nz, 7)), dma((nz, 7)), dma((nz, 3)), dma((nz, 3)), dma((1,)), dma((1,)),
         ],
         compiler_params=pltpu.CompilerParams(
             collective_id=0, has_side_effects=True, vmem_limit_bytes=48 * 1024 * 1024),

time: 50.3 us -> 48.7 us (0.968)
  Pallas kernels: 49.5 us -> 47.9 us
    pallas_call x1, Pallas kernels: 48.3 us -> 46.7 us  [fused(): pl.pallas_call(functools.partial(kernel, nz, n_sys, n_exp, rows, width),...]
where the time goes in v3:
time: 48.7 us; the launch traced here: 48.5 us
  Pallas kernels  47.9 us (98%)
  between operations  0.64 us (1%)
    pallas_call x1, Pallas kernels, fused(): pl.pallas_call(functools.partial(kernel, nz, n_sys, n_exp, rows, width),...  46.7 us
    pallas_call x1, Pallas kernels, fused(): pl.pallas_call(settle, out_shape=(jax.ShapeDtypeStruct(inputs.shape, BF16...  1.16 us

profile of v3, /device:TPU:0, one launch (start us, length us, event | category | flops | bytes accessed | tf_op | source)
XLA Modules:
  0.0 48.5 jit_solution(1193837300053594814)
XLA Ops:
  0.6 46.7 %shard_map.68 = (bf16[4,256,512]{2,1,0:T(8,128)(2,1)S(1)}, f32[256,512]{1,0:T(8,128)S(1)}) custom-call(s32[4]{0:T(128)} %counts_hbm.1, s32[4,16]{1,0:T(4,128)} %co_hbm.1, bf16[4,256,512]{2,1,0:T(8,128)(2,1)} %in_hbm.1, bf16[4,256,512]{2,1,0:T(8,128)(2,1)} %og_hbm.1, bf16[256,512]{1,0:T(8,128)(2,1)} %bitcast.2), custom_call_target="tpu_custom_call" | custom-call | tf_op jit(solution)/shard_map/pallas_call | solution.py:389
  47.3 1.2 %shard_map.69 = (bf16[4,256,512]{2,1,0:T(8,128)(2,1)}, f32[256,512]{1,0:T(8,128)}) custom-call(bf16[4,256,512]{2,1,0:T(8,128)(2,1)S(1)} %get-tuple-element.6.ig_ref, f32[256,512]{1,0:T(8,128)S(1)} %get-tuple-element.7.eg_ref), custom_call_target="tpu_custom_call" | custom-call | tf_op jit(solution)/shard_map/pallas_call | solution.py:435

commit v4 on v3

--- a/solution.py
+++ b/solution.py
@@ -21,7 +21,7 @@
 def kernel(nz, n_sys, n_exp, rows, width,
            counts_hbm, co_hbm, in_hbm, og_hbm, ex_hbm,
            ig_ref, eg_ref,
-           counts_ref, co_ref, in_ref, ex_ref, mk, cl, ca, ka, kt, kp, kq, pb, g, pc, gc, eo, zs, zr, xg, mb, mc, mr, mq, ps, pr,
+           counts_ref, co_ref, in_ref, ex_ref, mk, cl, ca, ka, kt, kp, kq, pb, g, pc, gc, eo, ec, zs, zr, zc, xg, xq, mb, mc, mr, mq, ps, pr,
            ld, loc, ka_s, ka_r, xp_s, xp_r, xz_s, xz_r, pb_s, pb_r, pc_s, pc_r, zs_s, zs_r,
            mb_s, mb_r, mc_s, mc_r, ps_s, ps_r):
     dp = lax.axis_index("dp")
@@ -31,9 +31,16 @@
     c = lax.rem(dp, 2)
     me = x * 4 + c * 2 + y
     sr = n_sys * rows
-    half_w = width // 2
+    half_w, quarter_w = width // 2, width // 4
     span = 8 * rows
     lo_cols, hi_cols = pl.ds(0, half_w), pl.ds(half_w, half_w)
+    second = slice(quarter_w, half_w)
+
+    def cut(near_z):
+        return quarter_w if near_z else half_w
+
+    def rest(near_z):
+        return slice(cut(near_z) - quarter_w, width - quarter_w)
 
     def flip(v, d):
         return lax.rem(v + d, 2)
@@ -138,6 +145,7 @@
     xp = send(own(1), xg.at[2, z], xp_s.at[0], xp_r.at[0], turned(1, 0, 0)[1])
     offer(0)
     offer(1)
+    xq_c = send(ex_ref.at[:, second], xq.at[0], xp_s.at[1], xp_r.at[1], turned(1, 0, 0)[1])
     ca_c = [send(cl, ca.at[me], ka_s.at[j - 1], ka_r.at[j - 1], near(j)[1]) for j in plane]
     ca_own = local(cl, ca.at[me])
 
@@ -158,70 +166,90 @@
 
     def produce(k):
         lanes = pl.ds(pl.multiple_of(target(k) * span, span), span)
+        n, others = cut(k >= 2), rest(k >= 2)
         for s in range(n_sys):
             prod = dot(in_ref[s, :, lanes], mk[s], 0, 0).astype(BF16)
             for b in range(8):
-                pb[b, k, s * rows:(s + 1) * rows, :] = prod[b * rows:(b + 1) * rows, :half_w]
-                pc[k, seat(b), s * rows:(s + 1) * rows, :] = prod[b * rows:(b + 1) * rows, half_w:]
+                pb[b, k, s * rows:(s + 1) * rows, :n] = prod[b * rows:(b + 1) * rows, :n]
+                pc[k, seat(b), s * rows:(s + 1) * rows, others] = prod[b * rows:(b + 1) * rows, n:]
         for v in (2, 3, 1):
             at = (p_at if v % 2 else q_at) * 2 + c
-            pc_c[k, v] = send(pc.at[k, 2 * v:2 * v + 2], gc.at[k, :, at], pc_s.at[k, v - 1], pc_r.at[k, v - 1],
+            pc_c[k, v] = send(pc.at[k, 2 * v:2 * v + 2, :, others], gc.at[k, :, at, :, others], pc_s.at[k, v - 1], pc_r.at[k, v - 1],
                               turned(*takers[v])[1])
-        gc_own[k] = local(pc.at[k, 0:2], gc.at[k, :, q_at * 2 + c])
+        gc_own[k] = local(pc.at[k, 0:2, :, others], gc.at[k, :, q_at * 2 + c, :, others])
 
     def deal(h):
-        two = slice(2 * h, 2 * h + 2)
+        two, n = slice(2 * h, 2 * h + 2), cut(h == 1)
         for j in plane:
             to, peer = near(j)
-            pb_c[h, j] = send(pb.at[to, two], g.at[two, me], pb_s.at[h, j - 1], pb_r.at[h, j - 1], peer)
-        g_own[h] = local(pb.at[me, two], g.at[two, me])
+            pb_c[h, j] = send(pb.at[to, two, :, :n], g.at[two, me, :, :n], pb_s.at[h, j - 1], pb_r.at[h, j - 1], peer)
+        g_own[h] = local(pb.at[me, two, :, :n], g.at[two, me, :, :n])
 
     mb_c, m_own, mc_c, mc_own = {}, {}, {}, {}
 
     def held(k, i):
         return ex_ref[:, (lo_cols, hi_cols)[i]] if k == 0 and i < 2 else xg[i, arrival(k)]
 
+    def mixed(weights, block):
+        return (dot(weights[0], block, 1, 0) + dot(weights[1], block, 1, 0)).astype(BF16)
+
     def merge(*ks):
         span_k = slice(ks[0], ks[-1] + 1)
+        close = ks[0] < 2
+        n, others = cut(close), rest(close)
         for k in ks:
             for i in (1, 2):
-                piece = held(k, i)
-                mc[:, :, k, flip(p_at, i - 1)] = (dot(kp[0], piece, 1, 0) + dot(kp[1], piece, 1, 0)).astype(
-                    BF16).reshape(4, n_sys, rows, half_w)
+                to = flip(p_at, i - 1)
+                mc[:, :, k, to, :, quarter_w:] = mixed(kp, held(k, i)).reshape(4, n_sys, rows, half_w)
+                if close:
+                    piece = xq[k] if i == 2 else held(k, 0)[:, second]
+                    mc[:, :, k, to, :, :quarter_w] = mixed(kp, piece).reshape(4, n_sys, rows, quarter_w)
         k = ks[-1]
         at = 2 * c + q_at
         for v, (fq, fc) in ((2, (1, 0)), (3, (1, 1)), (1, (0, 1))):
             u = flip(q_at, fq) * 2 + flip(c, fc)
-            mc_c[k, v] = send(mc.at[u, :, span_k], mq.at[:, span_k, at], mc_s.at[k, v - 1], mc_r.at[k, v - 1],
-                              turned(0, fq, fc)[1])
-        mc_own[k] = local(mc.at[q_at * 2 + c, :, span_k], mq.at[:, span_k, at])
+            mc_c[k, v] = send(mc.at[u, :, span_k, :, :, others], mq.at[:, span_k, at, :, :, others],
+                              mc_s.at[k, v - 1], mc_r.at[k, v - 1], turned(0, fq, fc)[1])
+        mc_own[k] = local(mc.at[q_at * 2 + c, :, span_k, :, :, others], mq.at[:, span_k, at, :, :, others])
         for k in ks:
-            piece = held(k, 0)
-            mb[:, :, k] = (dot(ka[0], piece, 1, 0) + dot(ka[1], piece, 1, 0)).astype(BF16).reshape(
-                8, n_sys, rows, half_w)
+            mb[:, :, k, :, :n] = mixed(ka, held(k, 0)[:, :n]).reshape(8, n_sys, rows, n)
         for j in plane:
             to, peer = near(j)
-            mb_c[k, j] = send(mb.at[to, :, span_k], mr.at[:, span_k, me], mb_s.at[k, j - 1], mb_r.at[k, j - 1], peer)
-        m_own[k] = local(mb.at[me, :, span_k], mr.at[:, span_k, me])
+            mb_c[k, j] = send(mb.at[to, :, span_k, :, :n], mr.at[:, span_k, me, :, :n],
+                              mb_s.at[k, j - 1], mb_r.at[k, j - 1], peer)
+        m_own[k] = local(mb.at[me, :, span_k, :, :n], mr.at[:, span_k, me, :, :n])
 
     def landed(slot, i):
         remote(zs.at[0, i], zr.at[slot, i], zs_s.at[0, i], zs_r.at[slot, i], line(1 - zm)).wait_recv()
         return zr[slot, i].astype(F32)
+
+    zc_c = []
 
     def reduce(k):
         gc_own[k].wait()
         for v in (1, 2, 3):
             pc_c[k, v].wait_recv()
         for i in (1, 0):
-            block = gc[k, i].reshape(4 * sr, half_w)
+            block = gc[k, i, :, :, quarter_w:].reshape(4 * sr, half_w)
             eo[k, i + 1] = dot(kq[0], block, 1, 0) + dot(kq[1], block, 1, 0)
             begin(k, i + 1)
+            if k >= 2:
+                block = gc[k, i, :, :, :quarter_w].reshape(4 * sr, quarter_w)
+                part = dot(kq[0], block, 1, 0) + dot(kq[1], block, 1, 0)
+                if i == 0:
+                    eo[k, 0, :, second] = part
+                elif k == 2:
+                    zc[0] = part.astype(BF16)
+                    zc_c.append(send(zc.at[0], zc.at[1], xp_s.at[3], xp_r.at[3], line(1 - zm)))
+                else:
+                    ec[...] = part
         if k % 2 == 0:
             g_own[k // 2].wait()
             for j in plane:
                 pb_c[k // 2, j].wait_recv()
-        block = g[k].reshape(8 * sr, half_w)
-        eo[k, 0] = dot(kt[0], block, 1, 0) + dot(kt[1], block, 1, 0)
+        n = cut(k >= 2)
+        block = g[k, :, :, :n].reshape(8 * sr, n)
+        eo[k, 0, :, :n] = dot(kt[0], block, 1, 0) + dot(kt[1], block, 1, 0)
         begin(k, 0)
 
     def onward(k, i):
@@ -252,9 +280,10 @@
                 mc_c[k, v].wait_recv()
         lanes = pl.ds(pl.multiple_of(arrival(k) * span, span), span)
         for s in range(n_sys):
-            first = mr[s, k].reshape(span, half_w)
-            last = jnp.concatenate([mq[s, k, (b % 2, 2 + b // 4)[b // 2 % 2], (b // 4, b % 2)[b // 2 % 2]]
-                                    for b in range(8)], axis=0)
+            first = mr[s, k, :, :, :cut(k < 2)].reshape(span, cut(k < 2))
+            last = jnp.concatenate(
+                [mq[s, k, (b % 2, 2 + b // 4)[b // 2 % 2], (b // 4, b % 2)[b // 2 % 2], :, rest(k < 2)]
+                 for b in range(8)], axis=0)
             ig_ref[s, :, lanes] = dot(mk[s], jnp.concatenate([first, last], axis=1), 1, 1).astype(BF16)
 
     def came(n, i):
@@ -283,6 +312,8 @@
     produce(2)
     produce(3)
     deal(1)
+    xq_c.wait_recv()
+    xq_n = send(xq.at[0], xq.at[1], xp_s.at[2], xp_r.at[2], line(1 - zm))
 
     ca_own.wait()
     for copy in ca_c:
@@ -318,6 +349,7 @@
     handed(2, 2)
     reduce(1)
     awaited(1)
+    xq_n.wait_recv()
     merge(0, 1)
     handed(3, 0)
     proceed(0, 2)
@@ -345,15 +377,18 @@
             eo[nz - 1, i] += landed(4, i)
 
     total(2)
-    ps[...] = eo[nz - 1, 2].astype(BF16)
+    zc_c[0].wait_recv()
+    ps[:, :quarter_w] = (ec[...] + zc[1].astype(F32)).astype(BF16)
+    ps[:, quarter_w:] = eo[nz - 1, 2].astype(BF16)
     ps_c = send(ps, pr, ps_s.at[0], ps_r.at[0], turned(1, 0, 0)[1])
     total(1)
     finish(2)
     total(0)
-    eg_ref[:, lo_cols] = eo[nz - 1, 0]
+    eg_ref[:, :quarter_w] = eo[nz - 1, 0, :, :quarter_w]
     finish(3)
     ps_c.wait_recv()
-    eg_ref[:, hi_cols] = eo[nz - 1, 1] + pr[...].astype(F32)
+    eg_ref[:, second] = eo[nz - 1, 0, :, second] + pr[:, :quarter_w].astype(F32)
+    eg_ref[:, hi_cols] = eo[nz - 1, 1] + pr[:, quarter_w:].astype(F32)
 
     for i in range(3):
         relay(i, own(0), z, 0, line(1 - zm)).wait_send()
@@ -382,7 +417,8 @@
     n_sys, n_slots, width = inputs.shape
     n_exp, rows, _ = experts.shape
     sr, er_rows = n_sys * rows, n_exp * rows
-    half_w = width // 2
+    half_w, quarter_w = width // 2, width // 4
+    most_w = width - quarter_w
     vmem = pl.BlockSpec(memory_space=pltpu.VMEM)
     hbm = pl.BlockSpec(memory_space=pltpu.HBM)
     dma = pltpu.SemaphoreType.DMA
@@ -408,20 +444,23 @@
             pltpu.VMEM((2, er_rows, 4 * sr), BF16),
             pltpu.VMEM((8, nz, sr, half_w), BF16),
             pltpu.VMEM((nz, 8, sr, half_w), BF16),
-            pltpu.VMEM((nz, 8, sr, half_w), BF16),
-            pltpu.VMEM((nz, 2, 4, sr, half_w), BF16),
+            pltpu.VMEM((nz, 8, sr, most_w), BF16),
+            pltpu.VMEM((nz, 2, 4, sr, most_w), BF16),
             pltpu.VMEM((nz, 3, er_rows, half_w), F32),
+            pltpu.VMEM((er_rows, quarter_w), F32),
             pltpu.VMEM((nz - 1, 3, er_rows, half_w), BF16),
             pltpu.VMEM((nz + 1, 3, er_rows, half_w), BF16),
+            pltpu.VMEM((2, er_rows, quarter_w), BF16),
             pltpu.VMEM((3, nz, er_rows, half_w), BF16),
+            pltpu.VMEM((2, er_rows, quarter_w), BF16),
             pltpu.VMEM((8, n_sys, nz, rows, half_w), BF16),
-            pltpu.VMEM((4, n_sys, nz, 2, rows, half_w), BF16),
+            pltpu.VMEM((4, n_sys, nz, 2, rows, most_w), BF16),
             pltpu.VMEM((n_sys, nz, 8, rows, half_w), BF16),
-            pltpu.VMEM((n_sys, nz, 4, 2, rows, half_w), BF16),
-            pltpu.VMEM((er_rows, half_w), BF16),
-            pltpu.VMEM((er_rows, half_w), BF16),
+            pltpu.VMEM((n_sys, nz, 4, 2, rows, most_w), BF16),
+            pltpu.VMEM((er_rows, most_w), BF16),
+            pltpu.VMEM((er_rows, most_w), BF16),
             dma((3 + 2 * n_sys,)), dma((1 + 4 * nz,)),
-            dma((7,)), dma((7,)), dma((1,)), dma((1,)), dma((3, nz + 1)), dma((3, nz)),
+            dma((7,)), dma((7,)), dma((4,)), dma((4,)), dma((3, nz + 1)), dma((3, nz)),
             dma((nz // 2, 7)), dma((nz // 2, 7)), dma((nz, 3)), dma((nz, 3)),
             dma((nz - 1, 3)), dma((nz + 1, 3)),
             dma((nz, 7)), dma((nz, 7)), dma((nz, 3)), dma((nz, 3)), dma((1,)), dma((1,)),
@@ -468,7 +507,7 @@
     def shards(inputs, out_grad, coeff_fixed, atom_counts, experts):
         n_sys, _, width = inputs.shape
         n_exp, rows, _ = experts.shape
-        if n_dp == 16 and n_fsdp == 2 and rows % 16 == 0 and n_sys <= 16 and n_exp <= 128 and width % 256 == 0:
+        if n_dp == 16 and n_fsdp == 2 and rows % 16 == 0 and n_sys <= 16 and n_exp <= 128 and width % 512 == 0:
             return fused(inputs, out_grad, coeff_fixed, atom_counts, experts, n_dp // 4)
         return plain(inputs, out_grad, coeff_fixed, atom_counts, experts)
 

time: 48.7 us -> 47.8 us (0.982)
  Pallas kernels: 47.9 us -> 47 us
    pallas_call x1, Pallas kernels: 46.7 us -> 45.8 us  [fused(): pl.pallas_call(functools.partial(kernel, nz, n_sys, n_exp, rows, width),...]
where the time goes in v4:
time: 47.8 us; the launch traced here: 47.6 us
  Pallas kernels  47 us (98%)
  between operations  0.64 us (1%)
    pallas_call x1, Pallas kernels, fused(): pl.pallas_call(functools.partial(kernel, nz, n_sys, n_exp, rows, width),...  45.8 us
    pallas_call x1, Pallas kernels, fused(): pl.pallas_call(settle, out_shape=(jax.ShapeDtypeStruct(inputs.shape, BF16...  1.16 us

profile of v4, /device:TPU:0, one launch (start us, length us, event | category | flops | bytes accessed | tf_op | source)
XLA Modules:
  0.0 47.6 jit_solution(5061161120197162661)
XLA Ops:
  0.6 45.8 %shard_map.68 = (bf16[4,256,512]{2,1,0:T(8,128)(2,1)S(1)}, f32[256,512]{1,0:T(8,128)S(1)}) custom-call(s32[4]{0:T(128)} %counts_hbm.1, s32[4,16]{1,0:T(4,128)} %co_hbm.1, bf16[4,256,512]{2,1,0:T(8,128)(2,1)} %in_hbm.1, bf16[4,256,512]{2,1,0:T(8,128)(2,1)} %og_hbm.1, bf16[256,512]{1,0:T(8,128)(2,1)} %bitcast.2), custom_call_target="tpu_custom_call" | custom-call | tf_op jit(solution)/shard_map/pallas_call | solution.py:425
  46.5 1.2 %shard_map.69 = (bf16[4,256,512]{2,1,0:T(8,128)(2,1)}, f32[256,512]{1,0:T(8,128)}) custom-call(bf16[4,256,512]{2,1,0:T(8,128)(2,1)S(1)} %get-tuple-element.6.ig_ref, f32[256,512]{1,0:T(8,128)S(1)} %get-tuple-element.7.eg_ref), custom_call_target="tpu_custom_call" | custom-call | tf_op jit(solution)/shard_map/pallas_call | solution.py:474

commit v5 on v4

--- a/solution.py
+++ b/solution.py
@@ -95,6 +95,47 @@
     og_c = [load(1 + s, og_hbm.at[s], mk.at[s]) for s in range(n_sys)]
     in_c = [load(1 + n_sys + s, in_hbm.at[s], in_ref.at[s]) for s in range(n_sys)]
 
+    ex_c.wait()
+    pl.semaphore_wait(barrier, len(peers) + zm)
+
+    def remote(src, dst, s, r, peer):
+        return pltpu.make_async_remote_copy(
+            src_ref=src, dst_ref=dst, send_sem=s, recv_sem=r, device_id=peer, device_id_type=MESH
+        )
+
+    sent = []
+
+    def send(src, dst, s, r, peer):
+        copy = remote(src, dst, s, r, peer)
+        copy.start()
+        sent.append(copy)
+        return copy
+
+    n_loc = [0]
+
+    def local(src, dst):
+        copy = pltpu.make_async_copy(src, dst, loc.at[n_loc[0]])
+        n_loc[0] += 1
+        copy.start()
+        return copy
+
+    def own(i):
+        return ex_ref.at[:, (lo_cols, hi_cols)[i]] if i < 2 else xg.at[2, z]
+
+    def relay(i, src, block, n, to):
+        return remote(src, xg.at[i, block], xz_s.at[i, n], xz_r.at[i, block], to)
+
+    def offer(i):
+        relay(i, own(i), z, 0, line(1 - zm)).start()
+
+        @pl.when(mid)
+        def _():
+            relay(i, own(i), z, nz, line(2)).start()
+
+    xp = send(own(1), xg.at[2, z], xp_s.at[0], xp_r.at[0], turned(1, 0, 0)[1])
+    offer(0)
+    offer(1)
+    xq_c = send(ex_ref.at[:, second], xq.at[0], xp_s.at[1], xp_r.at[1], turned(1, 0, 0)[1])
     col = lax.broadcasted_iota(jnp.int32, cl.shape[1:], 1)
     row = lax.broadcasted_iota(jnp.int32, cl.shape[1:], 0)
     fixed = jnp.zeros(cl.shape[1:], jnp.int32)
@@ -105,47 +146,6 @@
             fixed = jnp.where((row == s) & (col == e), co_ref[s, e], fixed)
     cl[0] = ((fixed >> 6).astype(F32) / 64.0).astype(BF16)
     cl[1] = ((fixed & 63).astype(F32) / 4096.0).astype(BF16)
-    ex_c.wait()
-    pl.semaphore_wait(barrier, len(peers) + zm)
-
-    def remote(src, dst, s, r, peer):
-        return pltpu.make_async_remote_copy(
-            src_ref=src, dst_ref=dst, send_sem=s, recv_sem=r, device_id=peer, device_id_type=MESH
-        )
-
-    sent = []
-
-    def send(src, dst, s, r, peer):
-        copy = remote(src, dst, s, r, peer)
-        copy.start()
-        sent.append(copy)
-        return copy
-
-    n_loc = [0]
-
-    def local(src, dst):
-        copy = pltpu.make_async_copy(src, dst, loc.at[n_loc[0]])
-        n_loc[0] += 1
-        copy.start()
-        return copy
-
-    def own(i):
-        return ex_ref.at[:, (lo_cols, hi_cols)[i]] if i < 2 else xg.at[2, z]
-
-    def relay(i, src, block, n, to):
-        return remote(src, xg.at[i, block], xz_s.at[i, n], xz_r.at[i, block], to)
-
-    def offer(i):
-        relay(i, own(i), z, 0, line(1 - zm)).start()
-
-        @pl.when(mid)
-        def _():
-            relay(i, own(i), z, nz, line(2)).start()
-
-    xp = send(own(1), xg.at[2, z], xp_s.at[0], xp_r.at[0], turned(1, 0, 0)[1])
-    offer(0)
-    offer(1)
-    xq_c = send(ex_ref.at[:, second], xq.at[0], xp_s.at[1], xp_r.at[1], turned(1, 0, 0)[1])
     ca_c = [send(cl, ca.at[me], ka_s.at[j - 1], ka_r.at[j - 1], near(j)[1]) for j in plane]
     ca_own = local(cl, ca.at[me])
 
@@ -383,9 +383,9 @@
     ps_c = send(ps, pr, ps_s.at[0], ps_r.at[0], turned(1, 0, 0)[1])
     total(1)
     finish(2)
+    finish(3)
     total(0)
     eg_ref[:, :quarter_w] = eo[nz - 1, 0, :, :quarter_w]
-    finish(3)
     ps_c.wait_recv()
     eg_ref[:, second] = eo[nz - 1, 0, :, second] + pr[:, :quarter_w].astype(F32)
     eg_ref[:, hi_cols] = eo[nz - 1, 1] + pr[:, quarter_w:].astype(F32)

time: 47.8 us -> 47.3 us (0.990)
  Pallas kernels: 47 us -> 46.5 us
where the time goes in v5:
time: 47.3 us; the launch traced here: 47.2 us
  Pallas kernels  46.5 us (98%)
  between operations  0.64 us (1%)
    pallas_call x1, Pallas kernels, fused(): pl.pallas_call(functools.partial(kernel, nz, n_sys, n_exp, rows, width),...  45.4 us
    pallas_call x1, Pallas kernels, fused(): pl.pallas_call(settle, out_shape=(jax.ShapeDtypeStruct(inputs.shape, BF16...  1.16 us

profile of v5, /device:TPU:0, one launch (start us, length us, event | category | flops | bytes accessed | tf_op | source)
XLA Modules:
  0.0 47.2 jit_solution(2190233155746102070)
XLA Ops:
  0.6 45.4 %shard_map.68 = (bf16[4,256,512]{2,1,0:T(8,128)(2,1)S(1)}, f32[256,512]{1,0:T(8,128)S(1)}) custom-call(s32[4]{0:T(128)} %counts_hbm.1, s32[4,16]{1,0:T(4,128)} %co_hbm.1, bf16[4,256,512]{2,1,0:T(8,128)(2,1)} %in_hbm.1, bf16[4,256,512]{2,1,0:T(8,128)(2,1)} %og_hbm.1, bf16[256,512]{1,0:T(8,128)(2,1)} %bitcast.2), custom_call_target="tpu_custom_call" | custom-call | tf_op jit(solution)/shard_map/pallas_call | solution.py:425
  46.0 1.2 %shard_map.69 = (bf16[4,256,512]{2,1,0:T(8,128)(2,1)}, f32[256,512]{1,0:T(8,128)}) custom-call(bf16[4,256,512]{2,1,0:T(8,128)(2,1)S(1)} %get-tuple-element.6.ig_ref, f32[256,512]{1,0:T(8,128)S(1)} %get-tuple-element.7.eg_ref), custom_call_target="tpu_custom_call" | custom-call | tf_op jit(solution)/shard_map/pallas_call | solution.py:474

commit v6 on v5

--- a/solution.py
+++ b/solution.py
@@ -21,7 +21,7 @@
 def kernel(nz, n_sys, n_exp, rows, width,
            counts_hbm, co_hbm, in_hbm, og_hbm, ex_hbm,
            ig_ref, eg_ref,
-           counts_ref, co_ref, in_ref, ex_ref, mk, cl, ca, ka, kt, kp, kq, pb, g, pc, gc, eo, ec, zs, zr, zc, xg, xq, mb, mc, mr, mq, ps, pr,
+           counts_ref, co_ref, in_ref, ex_ref, mk, cl, ca, ka, kt, kp, kq, pb, g, pc, gc, eo, zs, zr, xg, xq, mb, mc, mr, mq, ps, pr,
            ld, loc, ka_s, ka_r, xp_s, xp_r, xz_s, xz_r, pb_s, pb_r, pc_s, pc_r, zs_s, zs_r,
            mb_s, mb_r, mc_s, mc_r, ps_s, ps_r):
     dp = lax.axis_index("dp")
@@ -166,24 +166,24 @@
 
     def produce(k):
         lanes = pl.ds(pl.multiple_of(target(k) * span, span), span)
-        n, others = cut(k >= 2), rest(k >= 2)
+        n = half_w
         for s in range(n_sys):
             prod = dot(in_ref[s, :, lanes], mk[s], 0, 0).astype(BF16)
             for b in range(8):
-                pb[b, k, s * rows:(s + 1) * rows, :n] = prod[b * rows:(b + 1) * rows, :n]
-                pc[k, seat(b), s * rows:(s + 1) * rows, others] = prod[b * rows:(b + 1) * rows, n:]
+                pb[b, k, s * rows:(s + 1) * rows, :] = prod[b * rows:(b + 1) * rows, :n]
+                pc[k, seat(b), s * rows:(s + 1) * rows, :] = prod[b * rows:(b + 1) * rows, n:]
         for v in (2, 3, 1):
             at = (p_at if v % 2 else q_at) * 2 + c
-            pc_c[k, v] = send(pc.at[k, 2 * v:2 * v + 2, :, others], gc.at[k, :, at, :, others], pc_s.at[k, v - 1], pc_r.at[k, v - 1],
+            pc_c[k, v] = send(pc.at[k, 2 * v:2 * v + 2], gc.at[k, :, at], pc_s.at[k, v - 1], pc_r.at[k, v - 1],
                               turned(*takers[v])[1])
-        gc_own[k] = local(pc.at[k, 0:2, :, others], gc.at[k, :, q_at * 2 + c, :, others])
+        gc_own[k] = local(pc.at[k, 0:2], gc.at[k, :, q_at * 2 + c])
 
     def deal(h):
-        two, n = slice(2 * h, 2 * h + 2), cut(h == 1)
+        two = slice(2 * h, 2 * h + 2)
         for j in plane:
             to, peer = near(j)
-            pb_c[h, j] = send(pb.at[to, two, :, :n], g.at[two, me, :, :n], pb_s.at[h, j - 1], pb_r.at[h, j - 1], peer)
-        g_own[h] = local(pb.at[me, two, :, :n], g.at[two, me, :, :n])
+            pb_c[h, j] = send(pb.at[to, two], g.at[two, me], pb_s.at[h, j - 1], pb_r.at[h, j - 1], peer)
+        g_own[h] = local(pb.at[me, two], g.at[two, me])
 
     mb_c, m_own, mc_c, mc_own = {}, {}, {}, {}
 
@@ -223,33 +223,20 @@
         remote(zs.at[0, i], zr.at[slot, i], zs_s.at[0, i], zs_r.at[slot, i], line(1 - zm)).wait_recv()
         return zr[slot, i].astype(F32)
 
-    zc_c = []
-
     def reduce(k):
         gc_own[k].wait()
         for v in (1, 2, 3):
             pc_c[k, v].wait_recv()
         for i in (1, 0):
-            block = gc[k, i, :, :, quarter_w:].reshape(4 * sr, half_w)
+            block = gc[k, i].reshape(4 * sr, half_w)
             eo[k, i + 1] = dot(kq[0], block, 1, 0) + dot(kq[1], block, 1, 0)
             begin(k, i + 1)
-            if k >= 2:
-                block = gc[k, i, :, :, :quarter_w].reshape(4 * sr, quarter_w)
-                part = dot(kq[0], block, 1, 0) + dot(kq[1], block, 1, 0)
-                if i == 0:
-                    eo[k, 0, :, second] = part
-                elif k == 2:
-                    zc[0] = part.astype(BF16)
-                    zc_c.append(send(zc.at[0], zc.at[1], xp_s.at[3], xp_r.at[3], line(1 - zm)))
-                else:
-                    ec[...] = part
         if k % 2 == 0:
             g_own[k // 2].wait()
             for j in plane:
                 pb_c[k // 2, j].wait_recv()
-        n = cut(k >= 2)
-        block = g[k, :, :, :n].reshape(8 * sr, n)
-        eo[k, 0, :, :n] = dot(kt[0], block, 1, 0) + dot(kt[1], block, 1, 0)
+        block = g[k].reshape(8 * sr, half_w)
+        eo[k, 0] = dot(kt[0], block, 1, 0) + dot(kt[1], block, 1, 0)
         begin(k, 0)
 
     def onward(k, i):
@@ -377,18 +364,15 @@
             eo[nz - 1, i] += landed(4, i)
 
     total(2)
-    zc_c[0].wait_recv()
-    ps[:, :quarter_w] = (ec[...] + zc[1].astype(F32)).astype(BF16)
-    ps[:, quarter_w:] = eo[nz - 1, 2].astype(BF16)
+    ps[...] = eo[nz - 1, 2].astype(BF16)
     ps_c = send(ps, pr, ps_s.at[0], ps_r.at[0], turned(1, 0, 0)[1])
     total(1)
     finish(2)
     finish(3)
     total(0)
-    eg_ref[:, :quarter_w] = eo[nz - 1, 0, :, :quarter_w]
+    eg_ref[:, lo_cols] = eo[nz - 1, 0]
     ps_c.wait_recv()
-    eg_ref[:, second] = eo[nz - 1, 0, :, second] + pr[:, :quarter_w].astype(F32)
-    eg_ref[:, hi_cols] = eo[nz - 1, 1] + pr[:, quarter_w:].astype(F32)
+    eg_ref[:, hi_cols] = eo[nz - 1, 1] + pr[...].astype(F32)
 
     for i in range(3):
         relay(i, own(0), z, 0, line(1 - zm)).wait_send()
@@ -444,23 +428,21 @@
             pltpu.VMEM((2, er_rows, 4 * sr), BF16),
             pltpu.VMEM((8, nz, sr, half_w), BF16),
             pltpu.VMEM((nz, 8, sr, half_w), BF16),
-            pltpu.VMEM((nz, 8, sr, most_w), BF16),
-            pltpu.VMEM((nz, 2, 4, sr, most_w), BF16),
+            pltpu.VMEM((nz, 8, sr, half_w), BF16),
+            pltpu.VMEM((nz, 2, 4, sr, half_w), BF16),
             pltpu.VMEM((nz, 3, er_rows, half_w), F32),
-            pltpu.VMEM((er_rows, quarter_w), F32),
             pltpu.VMEM((nz - 1, 3, er_rows, half_w), BF16),
             pltpu.VMEM((nz + 1, 3, er_rows, half_w), BF16),
-            pltpu.VMEM((2, er_rows, quarter_w), BF16),
             pltpu.VMEM((3, nz, er_rows, half_w), BF16),
             pltpu.VMEM((2, er_rows, quarter_w), BF16),
             pltpu.VMEM((8, n_sys, nz, rows, half_w), BF16),
             pltpu.VMEM((4, n_sys, nz, 2, rows, most_w), BF16),
             pltpu.VMEM((n_sys, nz, 8, rows, half_w), BF16),
             pltpu.VMEM((n_sys, nz, 4, 2, rows, most_w), BF16),
-            pltpu.VMEM((er_rows, most_w), BF16),
-            pltpu.VMEM((er_rows, most_w), BF16),
+            pltpu.VMEM((er_rows, half_w), BF16),
+            pltpu.VMEM((er_rows, half_w), BF16),
             dma((3 + 2 * n_sys,)), dma((1 + 4 * nz,)),
-            dma((7,)), dma((7,)), dma((4,)), dma((4,)), dma((3, nz + 1)), dma((3, nz)),
+            dma((7,)), dma((7,)), dma((3,)), dma((3,)), dma((3, nz + 1)), dma((3, nz)),
             dma((nz // 2, 7)), dma((nz // 2, 7)), dma((nz, 3)), dma((nz, 3)),
             dma((nz - 1, 3)), dma((nz + 1, 3)),
             dma((nz, 7)), dma((nz, 7)), dma((nz, 3)), dma((nz, 3)), dma((1,)), dma((1,)),

time: 47.3 us -> 47.2 us (level)
  no operation moved by 1% of the time
where the time goes in v6:
time: 47.2 us; the launch traced here: 47.1 us
  Pallas kernels  46.4 us (98%)
  between operations  0.64 us (1%)
    pallas_call x1, Pallas kernels, fused(): pl.pallas_call(functools.partial(kernel, nz, n_sys, n_exp, rows, width),...  45.3 us
    pallas_call x1, Pallas kernels, fused(): pl.pallas_call(settle, out_shape=(jax.ShapeDtypeStruct(inputs.shape, BF16...  1.16 us

profile of v6, /device:TPU:0, one launch (start us, length us, event | category | flops | bytes accessed | tf_op | source)
XLA Modules:
  0.0 47.1 jit_solution(3466863830805515067)
XLA Ops:
  0.6 45.3 %shard_map.68 = (bf16[4,256,512]{2,1,0:T(8,128)(2,1)S(1)}, f32[256,512]{1,0:T(8,128)S(1)}) custom-call(s32[4]{0:T(128)} %counts_hbm.1, s32[4,16]{1,0:T(4,128)} %co_hbm.1, bf16[4,256,512]{2,1,0:T(8,128)(2,1)} %in_hbm.1, bf16[4,256,512]{2,1,0:T(8,128)(2,1)} %og_hbm.1, bf16[256,512]{1,0:T(8,128)(2,1)} %bitcast.2), custom_call_target="tpu_custom_call" | custom-call | tf_op jit(solution)/shard_map/pallas_call | solution.py:409
  45.9 1.2 %shard_map.69 = (bf16[4,256,512]{2,1,0:T(8,128)(2,1)}, f32[256,512]{1,0:T(8,128)}) custom-call(bf16[4,256,512]{2,1,0:T(8,128)(2,1)S(1)} %get-tuple-element.6.ig_ref, f32[256,512]{1,0:T(8,128)S(1)} %get-tuple-element.7.eg_ref), custom_call_target="tpu_custom_call" | custom-call | tf_op jit(solution)/shard_map/pallas_call | solution.py:456

commit v7 on v6

--- a/solution.py
+++ b/solution.py
@@ -136,16 +136,17 @@
     offer(0)
     offer(1)
     xq_c = send(ex_ref.at[:, second], xq.at[0], xp_s.at[1], xp_r.at[1], turned(1, 0, 0)[1])
-    col = lax.broadcasted_iota(jnp.int32, cl.shape[1:], 1)
-    row = lax.broadcasted_iota(jnp.int32, cl.shape[1:], 0)
-    fixed = jnp.zeros(cl.shape[1:], jnp.int32)
+    col = lax.broadcasted_iota(jnp.int32, cl.shape, 1)
+    row = lax.broadcasted_iota(jnp.int32, cl.shape, 0)
+    system = lax.rem(row, n_sys)
+    fixed = jnp.zeros(cl.shape, jnp.int32)
     co_c.wait()
     counts_c.wait()
     for s in range(n_sys):
         for e in range(n_exp):
-            fixed = jnp.where((row == s) & (col == e), co_ref[s, e], fixed)
-    cl[0] = ((fixed >> 6).astype(F32) / 64.0).astype(BF16)
-    cl[1] = ((fixed & 63).astype(F32) / 4096.0).astype(BF16)
+            fixed = jnp.where((system == s) & (col == e), co_ref[s, e], fixed)
+    high, low = (fixed >> 6).astype(F32) / 64.0, (fixed & 63).astype(F32) / 4096.0
+    cl[...] = jnp.where(row < n_sys, high, low).astype(BF16)
     ca_c = [send(cl, ca.at[me], ka_s.at[j - 1], ka_r.at[j - 1], near(j)[1]) for j in plane]
     ca_own = local(cl, ca.at[me])
 
@@ -306,16 +307,17 @@
     for copy in ca_c:
         copy.wait_recv()
     er_rows = n_exp * rows
-    lane = lax.broadcasted_iota(jnp.int32, (cl.shape[2], er_rows), 1)
-    first = lax.broadcasted_iota(jnp.int32, (cl.shape[2], er_rows), 0) * rows
+    lane = lax.broadcasted_iota(jnp.int32, (cl.shape[1], er_rows), 1)
+    first = lax.broadcasted_iota(jnp.int32, (cl.shape[1], er_rows), 0) * rows
     pick = jnp.where((lane >= first) & (lane < first + rows), 1.0, 0.0).astype(BF16)
-    wide = dot(ca[...].reshape(16 * cl.shape[1], cl.shape[2]), pick, 1, 0)
+    told = ca[...].astype(F32).reshape(8 * cl.shape[0], cl.shape[1]).astype(BF16)
+    wide = dot(told, pick, 1, 0)
     across = lax.broadcasted_iota(jnp.int32, (rows, er_rows), 1) % rows
     diagonal = across == lax.broadcasted_iota(jnp.int32, (rows, er_rows), 0)
     for d in range(8):
         for h in range(2):
             for s in range(n_sys):
-                at = (d * 2 + h) * cl.shape[1] + s
+                at = d * cl.shape[0] + h * n_sys + s
                 value = jnp.broadcast_to(wide[at:at + 1, :], (rows, er_rows))
                 spot = (d * n_sys + s) * rows
                 ka[h, spot:spot + rows, :] = jnp.where(diagonal, value, 0.0).astype(BF16)
@@ -420,8 +422,8 @@
             pltpu.VMEM(inputs.shape, BF16),
             pltpu.VMEM((er_rows, width), BF16),
             pltpu.VMEM(out_grad.shape, BF16),
-            pltpu.VMEM((2, 16, 128), BF16),
-            pltpu.VMEM((8, 2, 16, 128), BF16),
+            pltpu.VMEM((8, 128), BF16),
+            pltpu.VMEM((8, 8, 128), BF16),
             pltpu.VMEM((2, 8 * sr, er_rows), BF16),
             pltpu.VMEM((2, er_rows, 8 * sr), BF16),
             pltpu.VMEM((2, 4 * sr, er_rows), BF16),
@@ -489,7 +491,7 @@
     def shards(inputs, out_grad, coeff_fixed, atom_counts, experts):
         n_sys, _, width = inputs.shape
         n_exp, rows, _ = experts.shape
-        if n_dp == 16 and n_fsdp == 2 and rows % 16 == 0 and n_sys <= 16 and n_exp <= 128 and width % 512 == 0:
+        if n_dp == 16 and n_fsdp == 2 and rows % 16 == 0 and n_sys <= 4 and n_exp <= 128 and width % 512 == 0:
             return fused(inputs, out_grad, coeff_fixed, atom_counts, experts, n_dp // 4)
         return plain(inputs, out_grad, coeff_fixed, atom_counts, experts)
 

time: 47.2 us -> 46.7 us (0.989)
    pallas_call x1, Pallas kernels: 45.3 us -> 44.8 us  [fused(): pl.pallas_call(functools.partial(kernel, nz, n_sys, n_exp, rows, width),...]
where the time goes in v7:
time: 46.7 us; the launch traced here: 46.6 us
  Pallas kernels  46 us (99%)
  between operations  0.64 us (1%)
    pallas_call x1, Pallas kernels, fused(): pl.pallas_call(functools.partial(kernel, nz, n_sys, n_exp, rows, width),...  44.8 us
    pallas_call x1, Pallas kernels, fused(): pl.pallas_call(settle, out_shape=(jax.ShapeDtypeStruct(inputs.shape, BF16...  1.16 us

profile of v7, /device:TPU:0, one launch (start us, length us, event | category | flops | bytes accessed | tf_op | source)
XLA Modules:
  0.0 46.6 jit_solution(14240366156249245491)
XLA Ops:
  0.6 44.8 %shard_map.68 = (bf16[4,256,512]{2,1,0:T(8,128)(2,1)S(1)}, f32[256,512]{1,0:T(8,128)S(1)}) custom-call(s32[4]{0:T(128)} %counts_hbm.1, s32[4,16]{1,0:T(4,128)} %co_hbm.1, bf16[4,256,512]{2,1,0:T(8,128)(2,1)} %in_hbm.1, bf16[4,256,512]{2,1,0:T(8,128)(2,1)} %og_hbm.1, bf16[256,512]{1,0:T(8,128)(2,1)} %bitcast.2), custom_call_target="tpu_custom_call" | custom-call | tf_op jit(solution)/shard_map/pallas_call | solution.py:411
  45.4 1.2 %shard_map.69 = (bf16[4,256,512]{2,1,0:T(8,128)(2,1)}, f32[256,512]{1,0:T(8,128)}) custom-call(bf16[4,256,512]{2,1,0:T(8,128)(2,1)S(1)} %get-tuple-element.6.ig_ref, f32[256,512]{1,0:T(8,128)S(1)} %get-tuple-element.7.eg_ref), custom_call_target="tpu_custom_call" | custom-call | tf_op jit(solution)/shard_map/pallas_call | solution.py:458

commit v8 on v7

--- a/solution.py
+++ b/solution.py
@@ -12,6 +12,7 @@
 BF16 = jnp.bfloat16
 F32 = jnp.float32
 NEAR_ORDER = (5, 7, 4, 1, 6, 3, 2)
+DIAGONAL = (5, 7)
 
 
 def dot(a, b, ca, cb):
@@ -22,7 +23,7 @@
            counts_hbm, co_hbm, in_hbm, og_hbm, ex_hbm,
            ig_ref, eg_ref,
            counts_ref, co_ref, in_ref, ex_ref, mk, cl, ca, ka, kt, kp, kq, pb, g, pc, gc, eo, zs, zr, xg, xq, mb, mc, mr, mq, ps, pr,
-           ld, loc, ka_s, ka_r, xp_s, xp_r, xz_s, xz_r, pb_s, pb_r, pc_s, pc_r, zs_s, zs_r,
+           vouched, ld, loc, ka_s, ka_r, xp_s, xp_r, xz_s, xz_r, pb_s, pb_r, pc_s, pc_r, zs_s, zs_r,
            mb_s, mb_r, mc_s, mc_r, ps_s, ps_r):
     dp = lax.axis_index("dp")
     y = lax.axis_index("fsdp")
@@ -75,7 +76,7 @@
         return actual((3, 2, 1 - zm, zm)[n])
 
     plane = NEAR_ORDER
-    peers = [near(j)[1] for j in plane] + [line(1 - zm)]
+    peers = [near(j)[1] for j in plane if j not in DIAGONAL] + [line(1 - zm)]
     barrier = pltpu.get_barrier_semaphore()
     for peer in peers:
         pl.semaphore_signal(barrier, inc=1, device_id=peer, device_id_type=MESH)
@@ -132,6 +133,7 @@
         def _():
             relay(i, own(i), z, nz, line(2)).start()
 
+    pl.semaphore_signal(vouched, inc=1, device_id=near(4)[1], device_id_type=MESH)
     xp = send(own(1), xg.at[2, z], xp_s.at[0], xp_r.at[0], turned(1, 0, 0)[1])
     offer(0)
     offer(1)
@@ -147,7 +149,14 @@
             fixed = jnp.where((system == s) & (col == e), co_ref[s, e], fixed)
     high, low = (fixed >> 6).astype(F32) / 64.0, (fixed & 63).astype(F32) / 4096.0
     cl[...] = jnp.where(row < n_sys, high, low).astype(BF16)
-    ca_c = [send(cl, ca.at[me], ka_s.at[j - 1], ka_r.at[j - 1], near(j)[1]) for j in plane]
+    ca_c = []
+
+    def tell(j):
+        ca_c.append(send(cl, ca.at[me], ka_s.at[j - 1], ka_r.at[j - 1], near(j)[1]))
+
+    for j in plane:
+        if j not in DIAGONAL:
+            tell(j)
     ca_own = local(cl, ca.at[me])
 
     for s in range(n_sys):
@@ -296,6 +305,9 @@
     xp.wait_recv()
     offer(2)
     produce(1)
+    pl.semaphore_wait(vouched, 1)
+    for j in DIAGONAL:
+        tell(j)
     deal(0)
     produce(2)
     produce(3)
@@ -443,7 +455,7 @@
             pltpu.VMEM((n_sys, nz, 4, 2, rows, most_w), BF16),
             pltpu.VMEM((er_rows, half_w), BF16),
             pltpu.VMEM((er_rows, half_w), BF16),
-            dma((3 + 2 * n_sys,)), dma((1 + 4 * nz,)),
+            pltpu.SemaphoreType.REGULAR, dma((3 + 2 * n_sys,)), dma((1 + 4 * nz,)),
             dma((7,)), dma((7,)), dma((3,)), dma((3,)), dma((3, nz + 1)), dma((3, nz)),
             dma((nz // 2, 7)), dma((nz // 2, 7)), dma((nz, 3)), dma((nz, 3)),
             dma((nz - 1, 3)), dma((nz + 1, 3)),

time: 46.7 us -> 46.4 us (level)
  no operation moved by 1% of the time
where the time goes in v8:
time: 46.4 us; the launch traced here: 46.3 us
  Pallas kernels  45.7 us (98%)
  between operations  0.64 us (1%)
    pallas_call x1, Pallas kernels, fused(): pl.pallas_call(functools.partial(kernel, nz, n_sys, n_exp, rows, width),...  44.5 us
    pallas_call x1, Pallas kernels, fused(): pl.pallas_call(settle, out_shape=(jax.ShapeDtypeStruct(inputs.shape, BF16...  1.16 us

profile of v8, /device:TPU:0, one launch (start us, length us, event | category | flops | bytes accessed | tf_op | source)
XLA Modules:
  0.0 46.3 jit_solution(7420953112081164804)
XLA Ops:
  0.6 44.5 %shard_map.68 = (bf16[4,256,512]{2,1,0:T(8,128)(2,1)S(1)}, f32[256,512]{1,0:T(8,128)S(1)}) custom-call(s32[4]{0:T(128)} %counts_hbm.1, s32[4,16]{1,0:T(4,128)} %co_hbm.1, bf16[4,256,512]{2,1,0:T(8,128)(2,1)} %in_hbm.1, bf16[4,256,512]{2,1,0:T(8,128)(2,1)} %og_hbm.1, bf16[256,512]{1,0:T(8,128)(2,1)} %bitcast.2), custom_call_target="tpu_custom_call" | custom-call | tf_op jit(solution)/shard_map/pallas_call | solution.py:423
  45.1 1.2 %shard_map.69 = (bf16[4,256,512]{2,1,0:T(8,128)(2,1)}, f32[256,512]{1,0:T(8,128)}) custom-call(bf16[4,256,512]{2,1,0:T(8,128)(2,1)S(1)} %get-tuple-element.6.ig_ref, f32[256,512]{1,0:T(8,128)S(1)} %get-tuple-element.7.eg_ref), custom_call_target="tpu_custom_call" | custom-call | tf_op jit(solution)/shard_map/pallas_call | solution.py:470

commit v9 on v8

--- a/solution.py
+++ b/solution.py
@@ -96,7 +96,6 @@
     og_c = [load(1 + s, og_hbm.at[s], mk.at[s]) for s in range(n_sys)]
     in_c = [load(1 + n_sys + s, in_hbm.at[s], in_ref.at[s]) for s in range(n_sys)]
 
-    ex_c.wait()
     pl.semaphore_wait(barrier, len(peers) + zm)
 
     def remote(src, dst, s, r, peer):
@@ -121,7 +120,7 @@
         return copy
 
     def own(i):
-        return ex_ref.at[:, (lo_cols, hi_cols)[i]] if i < 2 else xg.at[2, z]
+        return ex_hbm.at[:, (lo_cols, hi_cols)[i]] if i < 2 else xg.at[2, z]
 
     def relay(i, src, block, n, to):
         return remote(src, xg.at[i, block], xz_s.at[i, n], xz_r.at[i, block], to)
@@ -137,7 +136,7 @@
     xp = send(own(1), xg.at[2, z], xp_s.at[0], xp_r.at[0], turned(1, 0, 0)[1])
     offer(0)
     offer(1)
-    xq_c = send(ex_ref.at[:, second], xq.at[0], xp_s.at[1], xp_r.at[1], turned(1, 0, 0)[1])
+    xq_c = send(ex_hbm.at[:, second], xq.at[0], xp_s.at[1], xp_r.at[1], turned(1, 0, 0)[1])
     col = lax.broadcasted_iota(jnp.int32, cl.shape, 1)
     row = lax.broadcasted_iota(jnp.int32, cl.shape, 0)
     system = lax.rem(row, n_sys)
@@ -315,6 +314,7 @@
     xq_c.wait_recv()
     xq_n = send(xq.at[0], xq.at[1], xp_s.at[2], xp_r.at[2], line(1 - zm))
 
+    ex_c.wait()
     ca_own.wait()
     for copy in ca_c:
         copy.wait_recv()

time: 46.4 us -> 46.3 us (level)
  no operation moved by 1% of the time
where the time goes in v9:
time: 46.3 us; the launch traced here: 46.2 us
  Pallas kernels  45.5 us (98%)
  between operations  0.64 us (1%)
    pallas_call x1, Pallas kernels, fused(): pl.pallas_call(functools.partial(kernel, nz, n_sys, n_exp, rows, width),...  44.4 us
    pallas_call x1, Pallas kernels, fused(): pl.pallas_call(settle, out_shape=(jax.ShapeDtypeStruct(inputs.shape, BF16...  1.16 us

profile of v9, /device:TPU:0, one launch (start us, length us, event | category | flops | bytes accessed | tf_op | source)
XLA Modules:
  0.0 46.2 jit_solution(13380007588084284539)
XLA Ops:
  0.6 44.4 %shard_map.68 = (bf16[4,256,512]{2,1,0:T(8,128)(2,1)S(1)}, f32[256,512]{1,0:T(8,128)S(1)}) custom-call(s32[4]{0:T(128)} %counts_hbm.1, s32[4,16]{1,0:T(4,128)} %co_hbm.1, bf16[4,256,512]{2,1,0:T(8,128)(2,1)} %in_hbm.1, bf16[4,256,512]{2,1,0:T(8,128)(2,1)} %og_hbm.1, bf16[256,512]{1,0:T(8,128)(2,1)} %bitcast.2), custom_call_target="tpu_custom_call" | custom-call | tf_op jit(solution)/shard_map/pallas_call | solution.py:423
  45.0 1.2 %shard_map.69 = (bf16[4,256,512]{2,1,0:T(8,128)(2,1)}, f32[256,512]{1,0:T(8,128)}) custom-call(bf16[4,256,512]{2,1,0:T(8,128)(2,1)S(1)} %get-tuple-element.6.ig_ref, f32[256,512]{1,0:T(8,128)S(1)} %get-tuple-element.7.eg_ref), custom_call_target="tpu_custom_call" | custom-call | tf_op jit(solution)/shard_map/pallas_call | solution.py:470
